TPU v7x, 128 devices: a whole 4x4x4 slice. The times are simulated.
128 devices in a mesh: region: 8 (over z, core), col: 16 (over x, y).
Axes of the slice: x: 4, y: 4, z: 4, core: 2. Of those that a mesh axis runs over, the one named last changes fastest.
Arguments:
- forcing: float32 [3, 512, 2048], P(None, 'region', 'col'), may hold values from 0.05 to 3
- river_storage: float32 [512, 2048], P('region', 'col'), may hold values from 0.1 to 4
- river_rate: float32 [512, 2048], P('region', 'col'), may hold values from 0.2 to 0.9
- flow_code: int32 [512, 2048], P('region', 'col'), may hold values from 1 to 128
- home_slot: int32 [128, 1024], P(('region', 'col')), may hold values from -1 to 1023, as said below
- home_offset: int32 [128, 1024], P(('region', 'col')), may hold values from 0 to 8184, as said below
- worker_list: int32 [61440], P(('region', 'col')), may hold values from 0 to 1023, as said below
- patch_cell: int32 [61440, 128], P(('region', 'col')), may hold values from 0 to 63, as said below
- patch_area: float32 [61440, 128], P(('region', 'col')), may hold values from 0.02 to 0.3
- canopy_water: float32 [61440, 128], P(('region', 'col')), may hold values from 0 to 1
- canopy_cap: float32 [61440, 128], P(('region', 'col')), may hold values from 0.1 to 2
- soil_water: float32 [15, 61440, 128], P(None, ('region', 'col')), may hold values from 0.05 to 0.5
- porosity: float32 [15, 61440, 128], P(None, ('region', 'col')), may hold values from 0.3 to 0.55
- drainage: float32 [15, 61440, 128], P(None, ('region', 'col')), may hold values from 0.02 to 0.8
Outputs:
- soil_new: float32 [15, 61440, 128], P(None, ('region', 'col'))
- canopy_new: float32 [61440, 128], P(('region', 'col'))
- cell_runoff: float32 [512, 2048], P('region', 'col')
- cell_evap: float32 [512, 2048], P('region', 'col')
- river_new: float32 [512, 2048], P('region', 'col')
Inputs may be any that keep to these rules, and one draw needn't show every extreme that they name: `home_slot`: A home's live block slots come first and hold w * 8 + k (worker w, position k), distinct within the home; -1 marks unused slots. A home has 1024, 512, 256 or 128 live blocks, each for a quarter of the homes; at most 8 of one home's blocks go to one worker, and the busiest homes send exactly 8 to every worker. `worker_list`: every slot of every worker holds a live block; h * 8 + k at block b of worker w means home_slot[h, j] = w * 8 + k for exactly one j. `home_offset`: the first home cell of a live block, row-major over the home's cells; 0 for unused slots. Offset plus patch_cell stays below 8192. `patch_cell`: never falling along a block.
All inputs are finite; a program needn't handle non-finite values.
Results may differ from a plain program's by a relative error of at most 0.000073.
Values sent between devices are 32-bit elements; how exact they have to be, the bound alone decides.
A program may use at most 64 MiB of HBM per device.

v0:
```python
import jax
import jax.numpy as jnp
from jax import lax
from jax.sharding import PartitionSpec as P

ITERS = 4


directions = ((0, 1), (1, 1), (1, 0), (1, -1), (0, -1), (-1, -1), (-1, 0), (-1, 1))
highest = lax.Precision.HIGHEST


def with_halo(value, sides, width):
    for axis, dim in sides:
        count, length = (lax.axis_size(axis), value.shape[dim])
        up = [(i, (i + 1) % count) for i in range(count - 1)]
        down = [(j, i) for i, j in up]
        last = lax.slice_in_dim(value, length - width, length, axis=dim)
        initial = lax.slice_in_dim(value, 0, width, axis=dim)
        before = lax.ppermute(last, axis, up)
        after = lax.ppermute(initial, axis, down)
        value = jnp.concatenate([before, value, after], axis=dim)
    return value


def inflow_from(out_pad, code_pad):
    inner_rows = out_pad.shape[0] - 2
    inner_cols = out_pad.shape[1] - 2
    arriving = jnp.zeros((inner_rows, inner_cols), jnp.float32)
    for code_bit, (row_step, col_step) in enumerate(directions):
        leaving_cell = jnp.where(code_pad == 1 << code_bit, out_pad, jnp.float32(0.0))
        arriving = (
            arriving
            + leaving_cell[
                1 - row_step : 1 - row_step + inner_rows, 1 - col_step : 1 - col_step + inner_cols
            ]
        )
    return arriving


def layer_pass(state_in, layer_in):
    flowing, surface = state_in
    content, pore_room, drain_rate = layer_in
    filled = content + flowing
    excess = jnp.maximum(filled - pore_room, 0.0)
    filled = filled - excess
    drained = drain_rate * filled
    return ((drained, surface + excess), filled - drained)


def land_step(
    rainfall, demand, soil_demand, canopy_water, canopy_cap, soil_water, porosity, drainage
):
    wetted = canopy_water + rainfall
    through = jnp.maximum(wetted - canopy_cap, 0.0)
    retained = jnp.minimum(wetted, canopy_cap)
    canopy_loss = jnp.minimum(demand, retained)
    canopy_new = retained - canopy_loss
    (bottom, surface), soil_mid = lax.scan(
        layer_pass, (through, jnp.zeros_like(through)), (soil_water, porosity, drainage)
    )
    soil_loss = jnp.minimum(jnp.minimum(soil_demand, demand - canopy_loss), 0.5 * soil_mid[0])
    soil_new = soil_mid.at[0].add(-soil_loss)
    return (canopy_new, soil_new, surface + bottom, canopy_loss + soil_loss)


def lane_shift(values, amount, leftward):
    shifted = values
    for bit_index in range(7):
        step_size = 1 << bit_index
        moved = jnp.roll(shifted, -step_size if leftward else step_size, axis=-1)
        taken = amount >> bit_index & 1 == 1
        shifted = jnp.where(taken[:, None, None], moved, shifted)
    return shifted


def shards(
    forcing,
    river_storage,
    river_rate,
    flow_code,
    home_slot,
    home_offset,
    worker_list,
    patch_cell,
    patch_area,
    canopy_water,
    canopy_cap,
    soil_water,
    porosity,
    drainage,
):
    region_count = lax.axis_size("region")
    column_count = lax.axis_size("col")
    home_count = region_count * column_count
    grid_rows, grid_cols = river_storage.shape
    cell_count = grid_rows * grid_cols
    lane_rows = cell_count // 128
    slot_count = home_slot.shape[1]
    capacity = slot_count // home_count
    width = 128
    slot_ids = home_slot[0]
    offsets = home_offset[0]
    row_start = offsets // 128
    lane_start = offsets % 128
    row_ids = jnp.arange(lane_rows + 1, dtype=jnp.int32)
    pick_low = (row_start[:, None] == row_ids[None, :]).astype(jnp.float32)
    pick_high = (row_start[:, None] + 1 == row_ids[None, :]).astype(jnp.float32)
    forcing_rows = jnp.concatenate(
        [jnp.transpose(forcing, (1, 0, 2)), jnp.zeros((1, 3, 128), jnp.float32)], axis=0
    )
    low_rows = jnp.einsum("jr,rvg->jvg", pick_low, forcing_rows, precision=highest)
    high_rows = jnp.einsum("jr,rvg->jvg", pick_high, forcing_rows, precision=highest)
    windows = lane_shift(jnp.concatenate([low_rows, high_rows], axis=2), lane_start, True)[
        :, :, :width
    ]
    slot_range = jnp.arange(slot_count, dtype=jnp.int32)
    place = (slot_ids[None, :] == slot_range[:, None]).astype(jnp.float32)
    outgoing = jnp.einsum("qj,jvg->qvg", place, windows, precision=highest)
    arrived = lax.all_to_all(
        outgoing.reshape(home_count, capacity * 3 * width),
        ("region", "col"),
        split_axis=0,
        concat_axis=0,
        tiled=True,
    )
    pick_block = (worker_list[:, None] == slot_range[None, :]).astype(jnp.float32)
    rows_in = jnp.einsum(
        "bq,qvg->bvg", pick_block, arrived.reshape(slot_count, 3, width), precision=highest
    )
    lane_index = jnp.arange(width, dtype=jnp.int32)
    onehot = (patch_cell[:, :, None] == lane_index[None, None, :]).astype(jnp.float32)
    patch_forcing = jnp.einsum("sig,svg->vsi", onehot, rows_in, precision=highest)
    canopy_new, soil_new, runoff, transpired = land_step(
        patch_forcing[0],
        patch_forcing[1],
        patch_forcing[2],
        canopy_water,
        canopy_cap,
        soil_water,
        porosity,
        drainage,
    )
    weighted = jnp.stack([patch_area * runoff, patch_area * transpired])
    partial_value = jnp.einsum("sig,vsi->svg", onehot, weighted, precision=highest)
    leaving = jnp.einsum("bq,bvg->qvg", pick_block, partial_value, precision=highest)
    returned = lax.all_to_all(
        leaving.reshape(home_count, capacity * 2 * width),
        ("region", "col"),
        split_axis=0,
        concat_axis=0,
        tiled=True,
    )
    per_slot = jnp.einsum(
        "qj,qvg->jvg", place, returned.reshape(slot_count, 2, width), precision=highest
    )
    widened = jnp.concatenate(
        [per_slot, jnp.zeros((slot_count, 2, 256 - width), jnp.float32)], axis=2
    )
    placed = lane_shift(widened, lane_start, False)
    totals = jnp.einsum(
        "jr,jvg->rvg", pick_low, placed[:, :, :128], precision=highest
    ) + jnp.einsum("jr,jvg->rvg", pick_high, placed[:, :, 128:], precision=highest)
    cell_runoff = totals[:lane_rows, 0]
    cell_evap = totals[:lane_rows, 1]
    storage = river_storage + cell_runoff
    code_pad = with_halo(flow_code, (("region", 0), ("col", 1)), 1)
    for sweep_index in range(ITERS):
        outflow = river_rate * storage
        out_pad = with_halo(outflow, (("region", 0), ("col", 1)), 1)
        storage = storage - outflow + inflow_from(out_pad, code_pad)
    return (soil_new, canopy_new, cell_runoff, cell_evap, storage)


def solution(mesh):
    placed = (
        P(None, "region", "col"),
        P("region", "col"),
        P("region", "col"),
        P("region", "col"),
        P(("region", "col"), None),
        P(("region", "col"), None),
        P(("region", "col")),
        P(("region", "col"), None),
        P(("region", "col"), None),
        P(("region", "col"), None),
        P(("region", "col"), None),
        P(None, ("region", "col"), None),
        P(None, ("region", "col"), None),
        P(None, ("region", "col"), None),
    )
    return jax.shard_map(
        shards,
        mesh=mesh,
        in_specs=placed,
        out_specs=(
            P(None, ("region", "col"), None),
            P(("region", "col"), None),
            P("region", "col"),
            P("region", "col"),
            P("region", "col"),
        ),
        check_vma=False,
    )
```

profile of v0, /device:TPU:38, one launch (start us, length us, event | category | flops | bytes accessed | tf_op | source)
XLA Modules:
  0.0 279.2 jit_solution(13570241592442314093)
XLA Ops:
  14.7 3.5 %fusion.8 = f32[1024,3,128]{2,0,1:T(8,128)S(1)} fusion(s32[1024]{0:T(1024)S(1)} %bitcast.105, f32[1024,3,256]{0,2,1:T(8,128)S(1)} %maximum_select_fusion.4, f32[1024,3,64]{0,2,1:T(8,128)S(1)} %slice.416, f32[1024,3,192]{0,2,1:T(8,128)S(1)} %slice.415, pred[1024]{0:T(1024)(128)(4,1)S(1)} %get-tuple-element.113), kind=kOutput, calls=%fused_computation.15 | convolution fusion | flops 4833673216 | bytes 6296576 | tf_op jit(solution)/shard_map/qj,jvg->qvg/dot_general | solution.py:119
  19.5 2.9 %all_to_all.16 = f32[128,1,3072]{2,1,0:T(1,128)} reshape(f32[1024,3,128]{2,1,0:T(4,128)S(1)} %copy.33) | data formatting | bytes 3145728 | tf_op jit(solution)/shard_map/all_to_all | solution.py:120
  22.3 10.2 %all-to-all-start = ((f32[128,1,3072]{2,1,0:T(1,128)}), f32[128,1,3072]{2,1,0:T(1,128)S(1)}, u32[]{:S(2)}, u32[]{:S(2)}) async-start(f32[128,1,3072]{2,1,0:T(1,128)} %all_to_all.16), calls=%async_computation | async-start | bytes 3145728 | tf_op jit(solution)/shard_map/all_to_all | solution.py:120
  32.6 21.5 %all-to-all-done = f32[128,1,3072]{2,1,0:T(1,128)S(1)} async-done(((f32[128,1,3072]{2,1,0:T(1,128)}), f32[128,1,3072]{2,1,0:T(1,128)S(1)}, u32[]{:S(2)}, u32[]{:S(2)}) %all-to-all-start) | async-done | bytes 1572896 | tf_op jit(solution)/shard_map/all_to_all | solution.py:120
  54.1 3.7 %reduce.2 = f32[128,3072]{1,0:T(8,128)S(1)} reduce(f32[128,1,3072]{2,1,0:T(1,128)S(1)} %all-to-all-done, f32[]{:T(128)} %constant.117), dimensions={1}, to_apply=%all_to_all.13.reduce_sub_computation | reduce | bytes 3145732 | tf_op jit(solution)/shard_map/all_to_all | solution.py:120
  57.9 2.2 reshape.186
  60.0 3.4 %fusion.17 = f32[480,3,128]{2,0,1:T(8,128)S(1)} fusion(f32[1024,3,128]{2,1,0:T(4,128)} %reshape.186, s32[480]{0:T(512)S(1)} %copy-done.6), kind=kOutput, calls=%fused_computation.39 | convolution fusion | flops 2265415680 | bytes 2312064 | tf_op jit(solution)/shard_map/bq,qvg->bvg/dot_general | solution.py:128
  63.5 31.0 %fusion.21 = f32[3,480,128]{2,0,1:T(4,128)S(1)} fusion(s32[480,128]{1,0:T(8,128)S(1)} %copy-done.7, f32[480,3,128]{2,0,1:T(8,128)S(1)} %fusion.17), kind=kOutput, calls=%fused_computation.44 | convolution fusion | flops 290979840 | bytes 1720320 | tf_op jit(solution)/shard_map/sig,svg->vsi/dot_general | solution.py:133
  95.1 48.2 %while.16 = (s32[]{:T(128)}, f32[480,128]{1,0:T(8,128)S(1)}, f32[480,128]{1,0:T(8,128)S(1)}, f32[15,480,128]{2,1,0:T(8,128)}, f32[15,480,128]{2,1,0:T(8,128)}, /...) while((s32[]{:T(128)}, f32[480,128]{1,0:T(8,128)S(1)}, ...), condition=%wide.region_1.2_spmd.clone, body=%wide.region_0.1_spmd.clone.sunk | while | flops 675843 | bytes 2703479 | solution.py:59
  96.3 2.0 bitcast_dynamic-update-slice_fusion.2
  99.5 2.0 bitcast_dynamic-update-slice_fusion.2
  102.7 2.0 bitcast_dynamic-update-slice_fusion.2
  105.9 2.0 bitcast_dynamic-update-slice_fusion.2
  109.2 2.0 bitcast_dynamic-update-slice_fusion.2
  112.4 2.0 bitcast_dynamic-update-slice_fusion.2
  115.6 2.0 bitcast_dynamic-update-slice_fusion.2
  118.8 2.0 bitcast_dynamic-update-slice_fusion.2
  122.0 2.0 bitcast_dynamic-update-slice_fusion.2
  125.2 2.0 bitcast_dynamic-update-slice_fusion.2
  128.4 2.0 bitcast_dynamic-update-slice_fusion.2
  131.6 2.0 bitcast_dynamic-update-slice_fusion.2
  134.8 2.0 bitcast_dynamic-update-slice_fusion.2
  138.1 2.0 bitcast_dynamic-update-slice_fusion.2
  141.3 2.0 bitcast_dynamic-update-slice_fusion.2
  144.4 22.3 %fusion.2 = f32[480,2,128]{2,1,0:T(2,128)S(1)} fusion(s32[480,128]{1,0:T(8,128)S(1)} %copy-done.7, f32[2,480,128]{2,1,0:T(8,128)S(1)} %pad_maximum_fusion.3), kind=kOutput, calls=%fused_computation.8 | convolution fusion | flops 196608000 | bytes 1228800 | tf_op jit(solution)/shard_map/sig,vsi->svg/dot_general | solution.py:145
  166.7 1.9 fusion.15
  170.5 7.8 %all-to-all-start.1 = ((f32[128,1,2048]{2,1,0:T(1,128)}), f32[128,1,2048]{2,1,0:T(1,128)S(1)}, u32[]{:S(2)}, u32[]{:S(2)}) async-start(f32[128,1,2048]{2,1,0:T(1,128)} %bitcast.15), calls=%async_computation.1 | async-start | bytes 2097152 | tf_op jit(solution)/shard_map/all_to_all | solution.py:147
  178.3 1.9 collective-permute-start.1
  180.2 2.4 collective-permute-start
  182.6 4.0 %collective-permute-done = s32[1,128]{1,0:T(1,128)S(1)} collective-permute-done((s32[1,128]{1,0:T(1,128)S(1)}, s32[1,128]{1,0:T(1,128)S(1)}, u32[]{:S(2)}, u32[]{:S(2)}) %collective-permute-start) | collective-permute-done | bytes 544 | tf_op jit(solution)/shard_map/ppermute | solution.py:20
  186.7 4.6 %collective-permute-start.3 = (s32[66,1]{1,0:T(8,128)S(1)}, s32[66,1]{1,0:T(8,128)S(1)}, u32[]{:S(2)}, u32[]{:S(2)}) collective-permute-start(s32[66,1]{1,0:T(8,128)S(1)} %get-tuple-element.135), channel_id=1, source_target_pairs={{1,0},{2,1},{3,2},{4,3},{5,4},{6,5},{7,6},{8,7},{9,8},{10,9},{11,1... | collective-permute-start | bytes 800 | tf_op jit(solution)/shard_map/ppermute | solution.py:21
  195.0 2.1 fusion.6
  204.5 3.9 %collective-permute-start.5 = (f32[1,128]{1,0:T(1,128)S(1)}, f32[1,128]{1,0:T(1,128)S(1)}, u32[]{:S(2)}, u32[]{:S(2)}) collective-permute-start(f32[1,128]{1,0:T(1,128)S(1)} %get-tuple-element.147), channel_id=1, source_target_pairs={{16,0},{32,16},{48,32},{64,48},{80,64},{96,80},{112,96},{17,1},{33... | collective-permute-start | bytes 1544 | tf_op jit(solution)/shard_map/ppermute | solution.py:21
  210.4 2.8 %collective-permute-done.4 = f32[1,128]{1,0:T(1,128)S(1)} collective-permute-done((f32[1,128]{1,0:T(1,128)S(1)}, f32[1,128]{1,0:T(1,128)S(1)}, u32[]{:S(2)}, u32[]{:S(2)}) %collective-permute-start.4) | collective-permute-done | bytes 544 | tf_op jit(solution)/shard_map/ppermute | solution.py:20
  213.3 5.8 %collective-permute-start.7 = (f32[66,1]{1,0:T(8,128)S(1)}, f32[66,1]{1,0:T(8,128)S(1)}, u32[]{:S(2)}, u32[]{:S(2)}) collective-permute-start(f32[66,1]{1,0:T(8,128)S(1)} %get-tuple-element.137), channel_id=1, source_target_pairs={{1,0},{2,1},{3,2},{4,3},{5,4},{6,5},{7,6},{8,7},{9,8},{10,9},{11,1... | collective-permute-start | bytes 800 | tf_op jit(solution)/shard_map/ppermute | solution.py:21
  219.1 1.9 collective-permute-start.6
  221.1 5.9 %collective-permute-done.6 = f32[66,1]{1,0:T(8,128)S(1)} collective-permute-done((f32[66,1]{1,0:T(8,128)S(1)}, f32[66,1]{1,0:T(8,128)S(1)}, u32[]{:S(2)}, u32[]{:S(2)}) %collective-permute-start.6) | collective-permute-done | bytes 296 | tf_op jit(solution)/shard_map/ppermute | solution.py:20
  229.3 2.4 collective-permute-start.8
  231.7 2.5 collective-permute-done.8
  236.2 3.9 %collective-permute-start.10 = (f32[66,1]{1,0:T(8,128)S(1)}, f32[66,1]{1,0:T(8,128)S(1)}, u32[]{:S(2)}, u32[]{:S(2)}) collective-permute-start(f32[66,1]{1,0:T(8,128)S(1)} %get-tuple-element.132), channel_id=1, source_target_pairs={{0,1},{1,2},{2,3},{3,4},{4,5},{5,6},{6,7},{7,8},{8,9},{9,10},{10,1... | collective-permute-start | bytes 800 | tf_op jit(solution)/shard_map/ppermute | solution.py:20
  240.1 4.0 %collective-permute-done.10 = f32[66,1]{1,0:T(8,128)S(1)} collective-permute-done((f32[66,1]{1,0:T(8,128)S(1)}, f32[66,1]{1,0:T(8,128)S(1)}, u32[]{:S(2)}, u32[]{:S(2)}) %collective-permute-start.10) | collective-permute-done | bytes 296 | tf_op jit(solution)/shard_map/ppermute | solution.py:20
  246.3 2.4 collective-permute-start.12
  248.8 2.5 collective-permute-done.12
  253.2 3.9 %collective-permute-start.14 = (f32[66,1]{1,0:T(8,128)S(1)}, f32[66,1]{1,0:T(8,128)S(1)}, u32[]{:S(2)}, u32[]{:S(2)}) collective-permute-start(f32[66,1]{1,0:T(8,128)S(1)} %get-tuple-element.130), channel_id=1, source_target_pairs={{0,1},{1,2},{2,3},{3,4},{4,5},{5,6},{6,7},{7,8},{8,9},{9,10},{10,1... | collective-permute-start | bytes 800 | tf_op jit(solution)/shard_map/ppermute | solution.py:20
  258.8 2.4 collective-permute-done.14
  263.4 2.4 collective-permute-start.16
  270.3 3.9 %collective-permute-start.18 = (f32[66,1]{1,0:T(8,128)S(1)}, f32[66,1]{1,0:T(8,128)S(1)}, u32[]{:S(2)}, u32[]{:S(2)}) collective-permute-start(f32[66,1]{1,0:T(8,128)S(1)} %get-tuple-element.128), channel_id=1, source_target_pairs={{0,1},{1,2},{2,3},{3,4},{4,5},{5,6},{6,7},{7,8},{8,9},{9,10},{10,1... | collective-permute-start | bytes 800 | tf_op jit(solution)/shard_map/ppermute | solution.py:20
  274.9 3.4 %collective-permute-done.18 = f32[66,1]{1,0:T(8,128)S(1)} collective-permute-done((f32[66,1]{1,0:T(8,128)S(1)}, f32[66,1]{1,0:T(8,128)S(1)}, u32[]{:S(2)}, u32[]{:S(2)}) %collective-permute-start.18) | collective-permute-done | bytes 296 | tf_op jit(solution)/shard_map/ppermute | solution.py:20
  (137 shorter events, 67.5 us)
Async XLA Ops:
  14.0 0.7 copy-start.8
  22.3 31.7 %all-to-all-start = ((f32[128,1,3072]{2,1,0:T(1,128)}), f32[128,1,3072]{2,1,0:T(1,128)S(1)}, u32[]{:S(2)}, u32[]{:S(2)}) async-start(f32[128,1,3072]{2,1,0:T(1,128)} %all_to_all.16), calls=%async_computation | async-start | bytes 3145728 | tf_op jit(solution)/shard_map/all_to_all | solution.py:120
  57.8 2.2 copy-start.6
  57.8 5.6 %copy-start.7 = (s32[480,128]{1,0:T(8,128)S(1)}, s32[480,128]{1,0:T(8,128)}, u32[]{:S(2)}) copy-start(s32[480,128]{1,0:T(8,128)} %param.25) | copy-start | bytes 737284
  63.4 31.6 %copy-start = (f32[480,128]{1,0:T(8,128)S(1)}, f32[480,128]{1,0:T(8,128)}, u32[]{:S(2)}) copy-start(f32[480,128]{1,0:T(8,128)} %param.28) | copy-start | bytes 737284
  63.4 31.6 %copy-start.1 = (f32[480,128]{1,0:T(8,128)S(1)}, f32[480,128]{1,0:T(8,128)}, u32[]{:S(2)}) copy-start(f32[480,128]{1,0:T(8,128)} %param.27) | copy-start | bytes 737284
  95.1 48.3 %copy-start.3 = (f32[480,128]{1,0:T(8,128)S(1)}, f32[480,128]{1,0:T(8,128)}, u32[]{:S(2)}) copy-start(f32[480,128]{1,0:T(8,128)} %param.26) | copy-start | bytes 737284
  168.6 9.6 %copy-start.4 = (s32[64,128]{1,0:T(8,128)S(1)}, s32[64,128]{1,0:T(8,128)}, u32[]{:S(2)}) copy-start(s32[64,128]{1,0:T(8,128)} %param.21) | copy-start | bytes 98308
  170.5 24.1 %all-to-all-start.1 = ((f32[128,1,2048]{2,1,0:T(1,128)}), f32[128,1,2048]{2,1,0:T(1,128)S(1)}, u32[]{:S(2)}, u32[]{:S(2)}) async-start(f32[128,1,2048]{2,1,0:T(1,128)} %bitcast.15), calls=%async_computation.1 | async-start | bytes 2097152 | tf_op jit(solution)/shard_map/all_to_all | solution.py:147
  178.3 4.3 %collective-permute-start.1 = (s32[1,128]{1,0:T(1,128)S(1)}, s32[1,128]{1,0:T(1,128)S(1)}, u32[]{:S(2)}, u32[]{:S(2)}) collective-permute-start(s32[1,128]{1,0:T(1,128)S(1)} %get-tuple-element.145), channel_id=1, source_target_pairs={{16,0},{32,16},{48,32},{64,48},{80,64},{96,80},{112,96},{17,1},{33... | collective-permute-start | bytes 1544 | tf_op jit(solution)/shard_map/ppermute | solution.py:21
  180.2 6.4 %collective-permute-start = (s32[1,128]{1,0:T(1,128)S(1)}, s32[1,128]{1,0:T(1,128)S(1)}, u32[]{:S(2)}, u32[]{:S(2)}) collective-permute-start(s32[1,128]{1,0:T(1,128)S(1)} %get-tuple-element.144), channel_id=1, source_target_pairs={{0,16},{16,32},{32,48},{48,64},{64,80},{80,96},{96,112},{1,17},{17... | collective-permute-start | bytes 1544 | tf_op jit(solution)/shard_map/ppermute | solution.py:20
  186.7 23.6 %collective-permute-start.3 = (s32[66,1]{1,0:T(8,128)S(1)}, s32[66,1]{1,0:T(8,128)S(1)}, u32[]{:S(2)}, u32[]{:S(2)}) collective-permute-start(s32[66,1]{1,0:T(8,128)S(1)} %get-tuple-element.135), channel_id=1, source_target_pairs={{1,0},{2,1},{3,2},{4,3},{5,4},{6,5},{7,6},{8,7},{9,8},{10,9},{11,1... | collective-permute-start | bytes 800 | tf_op jit(solution)/shard_map/ppermute | solution.py:21
  191.3 19.0 %collective-permute-start.2 = (s32[66,1]{1,0:T(8,128)S(1)}, s32[66,1]{1,0:T(8,128)S(1)}, u32[]{:S(2)}, u32[]{:S(2)}) collective-permute-start(s32[66,1]{1,0:T(8,128)S(1)} %get-tuple-element.134), channel_id=1, source_target_pairs={{0,1},{1,2},{2,3},{3,4},{4,5},{5,6},{6,7},{7,8},{8,9},{9,10},{10,1... | collective-permute-start | bytes 800 | tf_op jit(solution)/shard_map/ppermute | solution.py:20
  201.9 2.0 copy-start.2
  201.9 2.0 copy-start.5
  204.5 6.0 %collective-permute-start.5 = (f32[1,128]{1,0:T(1,128)S(1)}, f32[1,128]{1,0:T(1,128)S(1)}, u32[]{:S(2)}, u32[]{:S(2)}) collective-permute-start(f32[1,128]{1,0:T(1,128)S(1)} %get-tuple-element.147), channel_id=1, source_target_pairs={{16,0},{32,16},{48,32},{64,48},{80,64},{96,80},{112,96},{17,1},{33... | collective-permute-start | bytes 1544 | tf_op jit(solution)/shard_map/ppermute | solution.py:21
  208.4 4.9 %collective-permute-start.4 = (f32[1,128]{1,0:T(1,128)S(1)}, f32[1,128]{1,0:T(1,128)S(1)}, u32[]{:S(2)}, u32[]{:S(2)}) collective-permute-start(f32[1,128]{1,0:T(1,128)S(1)} %get-tuple-element.146), channel_id=1, source_target_pairs={{0,16},{16,32},{32,48},{48,64},{64,80},{80,96},{96,112},{1,17},{17... | collective-permute-start | bytes 1544 | tf_op jit(solution)/shard_map/ppermute | solution.py:20
  213.3 7.8 %collective-permute-start.7 = (f32[66,1]{1,0:T(8,128)S(1)}, f32[66,1]{1,0:T(8,128)S(1)}, u32[]{:S(2)}, u32[]{:S(2)}) collective-permute-start(f32[66,1]{1,0:T(8,128)S(1)} %get-tuple-element.137), channel_id=1, source_target_pairs={{1,0},{2,1},{3,2},{4,3},{5,4},{6,5},{7,6},{8,7},{9,8},{10,9},{11,1... | collective-permute-start | bytes 800 | tf_op jit(solution)/shard_map/ppermute | solution.py:21
  219.1 8.0 %collective-permute-start.6 = (f32[66,1]{1,0:T(8,128)S(1)}, f32[66,1]{1,0:T(8,128)S(1)}, u32[]{:S(2)}, u32[]{:S(2)}) collective-permute-start(f32[66,1]{1,0:T(8,128)S(1)} %get-tuple-element.136), channel_id=1, source_target_pairs={{0,1},{1,2},{2,3},{3,4},{4,5},{5,6},{6,7},{7,8},{8,9},{9,10},{10,1... | collective-permute-start | bytes 800 | tf_op jit(solution)/shard_map/ppermute | solution.py:20
  227.3 4.3 %collective-permute-start.9 = (f32[1,128]{1,0:T(1,128)S(1)}, f32[1,128]{1,0:T(1,128)S(1)}, u32[]{:S(2)}, u32[]{:S(2)}) collective-permute-start(f32[1,128]{1,0:T(1,128)S(1)} %get-tuple-element.143), channel_id=1, source_target_pairs={{16,0},{32,16},{48,32},{64,48},{80,64},{96,80},{112,96},{17,1},{33... | collective-permute-start | bytes 1544 | tf_op jit(solution)/shard_map/ppermute | solution.py:21
  229.3 4.9 %collective-permute-start.8 = (f32[1,128]{1,0:T(1,128)S(1)}, f32[1,128]{1,0:T(1,128)S(1)}, u32[]{:S(2)}, u32[]{:S(2)}) collective-permute-start(f32[1,128]{1,0:T(1,128)S(1)} %get-tuple-element.142), channel_id=1, source_target_pairs={{0,16},{16,32},{32,48},{48,64},{64,80},{80,96},{96,112},{1,17},{17... | collective-permute-start | bytes 1544 | tf_op jit(solution)/shard_map/ppermute | solution.py:20
  234.2 5.9 %collective-permute-start.11 = (f32[66,1]{1,0:T(8,128)S(1)}, f32[66,1]{1,0:T(8,128)S(1)}, u32[]{:S(2)}, u32[]{:S(2)}) collective-permute-start(f32[66,1]{1,0:T(8,128)S(1)} %get-tuple-element.133), channel_id=1, source_target_pairs={{1,0},{2,1},{3,2},{4,3},{5,4},{6,5},{7,6},{8,7},{9,8},{10,9},{11,1... | collective-permute-start | bytes 800 | tf_op jit(solution)/shard_map/ppermute | solution.py:21
  236.2 8.0 %collective-permute-start.10 = (f32[66,1]{1,0:T(8,128)S(1)}, f32[66,1]{1,0:T(8,128)S(1)}, u32[]{:S(2)}, u32[]{:S(2)}) collective-permute-start(f32[66,1]{1,0:T(8,128)S(1)} %get-tuple-element.132), channel_id=1, source_target_pairs={{0,1},{1,2},{2,3},{3,4},{4,5},{5,6},{6,7},{7,8},{8,9},{9,10},{10,1... | collective-permute-start | bytes 800 | tf_op jit(solution)/shard_map/ppermute | solution.py:20
  244.4 4.3 %collective-permute-start.13 = (f32[1,128]{1,0:T(1,128)S(1)}, f32[1,128]{1,0:T(1,128)S(1)}, u32[]{:S(2)}, u32[]{:S(2)}) collective-permute-start(f32[1,128]{1,0:T(1,128)S(1)} %get-tuple-element.141), channel_id=1, source_target_pairs={{16,0},{32,16},{48,32},{64,48},{80,64},{96,80},{112,96},{17,1},{33... | collective-permute-start | bytes 1544 | tf_op jit(solution)/shard_map/ppermute | solution.py:21
  246.3 4.9 %collective-permute-start.12 = (f32[1,128]{1,0:T(1,128)S(1)}, f32[1,128]{1,0:T(1,128)S(1)}, u32[]{:S(2)}, u32[]{:S(2)}) collective-permute-start(f32[1,128]{1,0:T(1,128)S(1)} %get-tuple-element.140), channel_id=1, source_target_pairs={{0,16},{16,32},{32,48},{48,64},{64,80},{80,96},{96,112},{1,17},{17... | collective-permute-start | bytes 1544 | tf_op jit(solution)/shard_map/ppermute | solution.py:20
  251.3 7.5 %collective-permute-start.15 = (f32[66,1]{1,0:T(8,128)S(1)}, f32[66,1]{1,0:T(8,128)S(1)}, u32[]{:S(2)}, u32[]{:S(2)}) collective-permute-start(f32[66,1]{1,0:T(8,128)S(1)} %get-tuple-element.131), channel_id=1, source_target_pairs={{1,0},{2,1},{3,2},{4,3},{5,4},{6,5},{7,6},{8,7},{9,8},{10,9},{11,1... | collective-permute-start | bytes 800 | tf_op jit(solution)/shard_map/ppermute | solution.py:21
  253.2 8.0 %collective-permute-start.14 = (f32[66,1]{1,0:T(8,128)S(1)}, f32[66,1]{1,0:T(8,128)S(1)}, u32[]{:S(2)}, u32[]{:S(2)}) collective-permute-start(f32[66,1]{1,0:T(8,128)S(1)} %get-tuple-element.130), channel_id=1, source_target_pairs={{0,1},{1,2},{2,3},{3,4},{4,5},{5,6},{6,7},{7,8},{8,9},{9,10},{10,1... | collective-permute-start | bytes 800 | tf_op jit(solution)/shard_map/ppermute | solution.py:20
  261.5 5.1 %collective-permute-start.17 = (f32[1,128]{1,0:T(1,128)S(1)}, f32[1,128]{1,0:T(1,128)S(1)}, u32[]{:S(2)}, u32[]{:S(2)}) collective-permute-start(f32[1,128]{1,0:T(1,128)S(1)} %get-tuple-element.139), channel_id=1, source_target_pairs={{16,0},{32,16},{48,32},{64,48},{80,64},{96,80},{112,96},{17,1},{33... | collective-permute-start | bytes 1544 | tf_op jit(solution)/shard_map/ppermute | solution.py:21
  263.4 4.9 %collective-permute-start.16 = (f32[1,128]{1,0:T(1,128)S(1)}, f32[1,128]{1,0:T(1,128)S(1)}, u32[]{:S(2)}, u32[]{:S(2)}) collective-permute-start(f32[1,128]{1,0:T(1,128)S(1)} %get-tuple-element.138), channel_id=1, source_target_pairs={{0,16},{16,32},{32,48},{48,64},{64,80},{80,96},{96,112},{1,17},{17... | collective-permute-start | bytes 1544 | tf_op jit(solution)/shard_map/ppermute | solution.py:20
  268.4 6.5 %collective-permute-start.19 = (f32[66,1]{1,0:T(8,128)S(1)}, f32[66,1]{1,0:T(8,128)S(1)}, u32[]{:S(2)}, u32[]{:S(2)}) collective-permute-start(f32[66,1]{1,0:T(8,128)S(1)} %get-tuple-element.129), channel_id=1, source_target_pairs={{1,0},{2,1},{3,2},{4,3},{5,4},{6,5},{7,6},{8,7},{9,8},{10,9},{11,1... | collective-permute-start | bytes 800 | tf_op jit(solution)/shard_map/ppermute | solution.py:21
  270.3 8.0 %collective-permute-start.18 = (f32[66,1]{1,0:T(8,128)S(1)}, f32[66,1]{1,0:T(8,128)S(1)}, u32[]{:S(2)}, u32[]{:S(2)}) collective-permute-start(f32[66,1]{1,0:T(8,128)S(1)} %get-tuple-element.128), channel_id=1, source_target_pairs={{0,1},{1,2},{2,3},{3,4},{4,5},{5,6},{6,7},{7,8},{8,9},{9,10},{10,1... | collective-permute-start | bytes 800 | tf_op jit(solution)/shard_map/ppermute | solution.py:20
where the time goes:
time: 281 us; the launch traced here: 279 us
  starting transfers between devices  72.8 us (26%)
  other arithmetic  69.3 us (25%)
  matrix products  69 us (25%)
  waiting for transfers between devices  52 us (19%)
  local copies, waits for them, and re-layouts  14.4 us (5%)
    dot_general x1, matrix products, shards(): jnp.einsum('sig,svg->vsi', onehot, rows_in, precision=highest)  31 us
    dynamic_update_slice x15, other arithmetic, land_step(): lax.scan(layer_pass, (through, jnp.zeros_like(through)), (soil_water, por...  30.6 us
    ppermute x10, waiting for transfers between devices, with_halo(): before = lax.ppermute(last, axis, up)  29.2 us
    ppermute x10, starting transfers between devices, with_halo(): after = lax.ppermute(initial, axis, down)  27.7 us
    ppermute x10, starting transfers between devices, with_halo(): before = lax.ppermute(last, axis, up)  27.1 us
    dot_general x1, matrix products, shards(): jnp.einsum('sig,vsi->svg', onehot, weighted, precision=highest)  22.3 us
    all_to_all x1, waiting for transfers between devices, shards(): lax.all_to_all(outgoing.reshape(home_count, capacity * 3 * width), ('regi...  21.5 us
    add x15, other arithmetic, layer_pass(): return ((drained, surface + excess), filled - drained)  17.6 us
  transfers between devices with their start and end apart: 22, of which 11 were waited for; matrix products, arithmetic and copies ran while one was open for 5% of the time, Pallas kernels for 0%

commit v1 on v0

v1 whole, which is shorter than its diff:
```python
import functools

import jax
import jax.numpy as jnp
from jax import lax
from jax.experimental import pallas as pl
from jax.experimental.pallas import tpu as pltpu
from jax.sharding import PartitionSpec as P

ITERS = 4
LANES = 128
SPAN = 64
ORDER = 37
CHUNK = 32
MESH = pl.DeviceIdType.MESH
f32, bf16, i32 = jnp.float32, jnp.bfloat16, jnp.int32


def iota(shape, dim):
    return lax.broadcasted_iota(i32, shape, dim)


def lane_take(values, index):
    numbers = lax.GatherDimensionNumbers(
        offset_dims=(),
        collapsed_slice_dims=(1,),
        start_index_map=(1,),
        operand_batching_dims=(0,),
        start_indices_batching_dims=(0,),
    )
    return lax.gather(
        values,
        index[..., None],
        numbers,
        slice_sizes=(1, 1),
        mode=lax.GatherScatterMode.PROMISE_IN_BOUNDS,
    )


def split3(value):
    high = value.astype(bf16)
    rest = value - high.astype(f32)
    middle = rest.astype(bf16)
    low = (rest - middle.astype(f32)).astype(bf16)
    return high, middle, low


def hot(mask):
    return jnp.where(mask, 1.0, 0.0).astype(bf16)


def dot(lhs, rhs):
    return lax.dot_general(
        lhs, rhs, (((1,), (0,)), ((), ())), preferred_element_type=f32
    )


def dot_nt(lhs, rhs):
    return lax.dot_general(
        lhs, rhs, (((1,), (1,)), ((), ())), preferred_element_type=f32
    )


def step_shift(step, n_row, n_col):
    code = (step * ORDER) % (n_row * n_col)
    return code // n_col, code % n_col


def locate_slots(me_r, me_c, n_row, n_col, slot, offset, rows, lanes):
    slots = slot.shape[1]
    part = 2 * LANES
    weight = jnp.where(
        iota((part, slots), 0) < LANES,
        lax.shift_right_logical(offset, 7),
        offset & (LANES - 1),
    )
    weight = weight.astype(f32).astype(bf16)
    for first in range(0, slots, part):
        index = iota((part, LANES), 0) + first
        step = lax.shift_right_logical(index, 3)
        code = (step * ORDER) & (n_row * n_col - 1)
        shift_r = lax.shift_right_logical(code, n_col.bit_length() - 1)
        shift_c = code & (n_col - 1)
        worker = ((me_r + shift_r) & (n_row - 1)) * n_col + ((me_c + shift_c) & (n_col - 1))
        wanted = worker * 8 + (index & 7)
        pick = jnp.concatenate(
            [hot(slot[:, l : l + LANES] == wanted) for l in range(0, slots, LANES)], axis=1
        )
        place = dot_nt(pick, weight)
        rows[first : first + part, :] = place[:, :LANES]
        lanes[first : first + part, :] = place[:, LANES:].astype(i32)


def cut_windows(forcing, rows, lanes, weight, windows):
    grid_rows = forcing.shape[1]
    for v in range(3):
        field = forcing[v]
        below = pltpu.roll(field, grid_rows - 1, 0)
        for d, (a, b) in enumerate(zip(split3(field), split3(below))):
            at = slice(d * grid_rows, (d + 1) * grid_rows)
            weight[at, v * LANES : (v + 1) * LANES] = a
            weight[at, (3 + v) * LANES : (4 + v) * LANES] = b
    weight[3 * grid_rows :, :] = jnp.zeros((4 * LANES // 2 - 3 * grid_rows, 6 * LANES), bf16)
    part = 2 * LANES
    lane = iota((part, LANES), 1)
    for first in range(0, rows.shape[0], part):
        at = slice(first, first + part)
        pick = hot(rows[at, :] == (lane & (grid_rows - 1)).astype(f32))
        both = dot(jnp.concatenate([pick, pick], axis=1), weight[...])
        start = lanes[at, :]
        index = ((lane & (SPAN - 1)) + start) & (LANES - 1)
        cut = []
        for v in range(3):
            near = both[:, v * LANES : (v + 1) * LANES]
            far = both[:, (3 + v) * LANES : (4 + v) * LANES]
            cut.append(lane_take(jnp.where(lane >= start, near, far), index))
        left = lane < SPAN
        pair = jnp.where(left, cut[0], cut[1])
        last = jnp.where(left, cut[2], pltpu.roll(cut[2], part - 4, 0))
        steps = slice(first // 8, (first + part) // 8)
        windows[steps, 0:8, :] = pair.reshape(part // 8, 8, LANES)
        windows[steps, 8:12, :] = last.reshape(part // 8, 8, LANES)[:, 0:4, :]


def block_pickers(listed, pick_rows, pick_slots):
    blocks = listed.shape[1]
    slots = pick_slots.shape[0]
    part = 2 * LANES
    for first in range(0, slots, part):
        row = iota((part, blocks), 0) + first
        pick_slots[first : first + part, :] = hot(row == listed)
    for first in range(0, blocks, LANES):
        size = min(LANES, blocks - first)
        column = jnp.broadcast_to(listed[:, first : first + size], (LANES, size)).T
        for l in range(0, slots, LANES):
            pick_rows[first : first + size, l : l + LANES] = hot(
                column == iota((size, LANES), 1) + l
            )


def segment_tables(at, cells, last_of, run):
    cell = cells[at, :]
    lane = iota(cell.shape, 1)
    wanted = lane & (SPAN - 1)
    place = jnp.zeros_like(lane)
    for step in (64, 32, 16, 8, 4, 2, 1):
        tried = place + step
        place = jnp.where(lane_take(cell, tried) <= wanted, tried, place)
    found = lane_take(cell, place) == wanted
    last_of[at, :] = jnp.where(found, place, place + LANES)
    start = jnp.where((lane == 0) | (pltpu.roll(cell, 1, 1) != cell), lane, 0)
    for step in (1, 2, 4, 8, 16, 32, 64):
        start = jnp.maximum(start, jnp.where(lane >= step, pltpu.roll(start, step, 1), 0))
    run[at, :] = lane - start


def gather_rows(arrived, pick_rows, parts, found):
    homes = arrived.shape[0]
    part = 2 * LANES
    for first in range(0, homes * 8, part):
        steps = slice(first // 8, (first + part) // 8)
        pair = arrived[steps, 0:8, :].reshape(part, LANES)
        half = arrived[steps, 8:12, :]
        last = jnp.concatenate([half, pltpu.roll(half, SPAN, 2)], axis=1).reshape(part, LANES)
        for d, (a, b) in enumerate(zip(split3(pair), split3(last))):
            parts[d, first : first + part, :LANES] = a
            parts[d, first : first + part, LANES:] = b
    pick = pick_rows[...]
    found[...] = dot(pick, parts[0]) + (dot(pick, parts[1]) + dot(pick, parts[2]))


def land_rows(
    at, found, cells, last_of, run, area, canopy_water, canopy_cap, canopy_out, soil, porosity, drainage, sums
):
    layers = soil.shape[0]
    cell = cells[at, :]
    lane = iota(cell.shape, 1)
    pair = found[at, :LANES]
    rainfall = lane_take(pair, cell)
    demand = lane_take(pair, cell + SPAN)
    soil_demand = lane_take(found[at, LANES:], cell)
    wetted = canopy_water[at, :] + rainfall
    cap = canopy_cap[at, :]
    flowing = jnp.maximum(wetted - cap, 0.0)
    retained = jnp.minimum(wetted, cap)
    canopy_loss = jnp.minimum(demand, retained)
    canopy_out[at, :] = retained - canopy_loss
    surface = jnp.zeros_like(flowing)
    transpired = canopy_loss
    for l in range(layers):
        filled = soil[l, at, :] + flowing
        excess = jnp.maximum(filled - porosity[l, at, :], 0.0)
        surface = surface + excess
        filled = filled - excess
        flowing = drainage[l, at, :] * filled
        kept = filled - flowing
        if l == 0:
            soil_loss = jnp.minimum(jnp.minimum(soil_demand, demand - canopy_loss), 0.5 * kept)
            kept = kept - soil_loss
            transpired = canopy_loss + soil_loss
        soil[l, at, :] = kept
    weight = area[at, :]
    runoff = weight * (surface + flowing)
    evap = weight * transpired
    before = run[at, :]
    for step in (1, 2, 4, 8, 16, 32, 64):
        same = before >= step
        runoff = runoff + jnp.where(same, pltpu.roll(runoff, step, 1), 0.0)
        evap = evap + jnp.where(same, pltpu.roll(evap, step, 1), 0.0)
    place = last_of[at, :]
    index = place & (LANES - 1)
    total = jnp.where(lane < SPAN, lane_take(runoff, index), lane_take(evap, index))
    total = jnp.where(place < LANES, total, 0.0)
    for d, piece in enumerate(split3(total)):
        sums[at, d * LANES : (d + 1) * LANES] = piece


def return_rows(pick_slots, sums, leaving):
    part = 2 * LANES
    for first in range(0, pick_slots.shape[0], part):
        three = dot(pick_slots[first : first + part, :], sums[...])
        total = three[:, :LANES] + (three[:, LANES : 2 * LANES] + three[:, 2 * LANES :])
        leaving[first // 8 : (first + part) // 8, :, :] = total.reshape(part // 8, 8, LANES)


def home_picker(rows, pick_cells):
    grid_rows = pick_cells.shape[0]
    for first in range(0, rows.shape[0], LANES):
        across = rows[first : first + LANES, :].T[:grid_rows, :]
        pick_cells[:, first : first + LANES] = hot(
            across == iota((grid_rows, LANES), 0).astype(f32)
        )


def place_sums(back, lanes, pick_cells):
    part = 2 * LANES
    grid_rows = pick_cells.shape[0]
    lane = iota((part, LANES), 1)
    total = jnp.zeros((grid_rows, 4 * LANES), f32)
    for first in range(0, pick_cells.shape[1], part):
        at = slice(first, first + part)
        sent = back[first // 8 : (first + part) // 8, :, :].reshape(part, LANES)
        start = lanes[at, :]
        index = (lane - start) & (LANES - 1)
        inside = index < SPAN
        near = inside & (lane >= start)
        far = inside & (lane < start)
        runoff = lane_take(sent, index)
        evap = lane_take(sent, (index + SPAN) & (LANES - 1))
        spread = jnp.concatenate(
            [
                jnp.where(near, runoff, 0.0),
                jnp.where(near, evap, 0.0),
                jnp.where(far, runoff, 0.0),
                jnp.where(far, evap, 0.0),
            ],
            axis=1,
        )
        high, middle, low = split3(spread)
        pick = pick_cells[:, at]
        total = total + (dot(pick, high) + (dot(pick, middle) + dot(pick, low)))
    first_row = iota((grid_rows, 2 * LANES), 0) == 0
    carried = pltpu.roll(total[:, 2 * LANES :], 1, 0)
    total = total[:, : 2 * LANES] + jnp.where(first_row, 0.0, carried)
    return total[:, :LANES], total[:, LANES:]


def pack_edges(field):
    lane = iota((8, LANES), 1)
    packed = jnp.zeros((8, LANES), field.dtype)
    for i in range(field.shape[0] // 8):
        piece = field[8 * i : 8 * i + 8, :]
        first = pltpu.roll(piece, 4 * i, 1) if i else piece
        last = pltpu.roll(piece, (SPAN + 4 * i + 4) % LANES, 1)
        packed = jnp.where((lane >= 4 * i) & (lane < 4 * i + 4), first, packed)
        packed = jnp.where((lane >= SPAN + 4 * i) & (lane < SPAN + 4 * i + 4), last, packed)
    return packed


def extend(field, halo, inside):
    up, down, left, right = inside
    lane = iota((8, LANES), 1)
    on_right = (lane < 4) & right
    on_left = (lane >= LANES - 4) & left

    def side(from_right, from_left):
        return jnp.where(on_right, from_right, jnp.where(on_left, from_left, 0.0))

    centre = jnp.concatenate(
        [jnp.where(up, halo[0], 0.0), field, jnp.where(down, halo[1], 0.0)], axis=0
    )
    sides = [jnp.where(up, side(halo[5], halo[4]), 0.0)]
    for i in range(field.shape[0] // 8):
        from_right = pltpu.roll(halo[3], LANES - 4 * i, 1) if i else halo[3]
        from_left = pltpu.roll(halo[2], LANES - 4 - (SPAN + 4 * i), 1) if 4 * i < SPAN - 4 else halo[2]
        sides.append(side(from_right, from_left))
    sides.append(jnp.where(down, side(halo[7], halo[6]), 0.0))
    return centre, jnp.concatenate(sides, axis=0)


def route(storage, rate, code):
    height = storage[0].shape[0]
    lane = iota(storage[0].shape, 1)

    def across(pair, east):
        centre, side = (pltpu.roll(x, 1 if east else LANES - 1, 1) for x in pair)
        edge = lane == (0 if east else LANES - 1)
        return jnp.where(edge, side, centre), jnp.where(edge, centre, side)

    def inflow(outflow):
        def from_row(step, column):
            bits = {
                (0, 1): 1, (1, 1): 2, (1, 0): 4, (1, -1): 8,
                (0, -1): 16, (-1, -1): 32, (-1, 0): 64, (-1, 1): 128,
            }
            if (step, column) == (0, 0):
                return None
            bit = float(bits[step, column])
            return [jnp.where(c == bit, o, 0.0) for c, o in zip(code, outflow)]

        total = None
        for column in (1, 0, -1):
            gathered = None
            for step in (1, -1, 0):
                moved = from_row(step, column)
                if moved is None:
                    continue
                if step:
                    moved = [pltpu.roll(x, 1 if step > 0 else height - 1, 0) for x in moved]
                gathered = moved if gathered is None else [a + b for a, b in zip(gathered, moved)]
            if column:
                gathered = across(gathered, column > 0)
            total = list(gathered) if total is None else [a + b for a, b in zip(total, gathered)]
        return total

    for _ in range(ITERS):
        outflow = [a * b for a, b in zip(rate, storage)]
        storage = [s - o + n for s, o, n in zip(storage, outflow, inflow(outflow))]
    return storage[0]


def step_kernel(
    n_row,
    n_col,
    forcing_h, storage_h, rate_h, code_h, slot_h, offset_h, list_h,
    cell_h, area_h, water_h, cap_h, soil_h, porosity_h, drainage_h,
    soil_o, canopy_o, runoff_o, evap_o, river_o,
    forcing, storage, rate, code, slot, offset, listed,
    cells, area, water, cap, canopy, soil, porosity, drainage,
    rows, lanes, weight, windows, arrived, pick_rows, pick_slots, pick_cells,
    last_of, run, parts, found, sums, leaving, back,
    fixed_edge, fixed_halo, edge, halo,
    load_sem, store_sem, fixed_sem, edge_sem, out_sem, back_sem,
):
    me_r, me_c = lax.axis_index("region"), lax.axis_index("col")
    me = me_r * n_col + me_c
    devices = n_row * n_col

    def peer(step, sign):
        shift_r, shift_c = step_shift(step, n_row, n_col)
        if sign > 0:
            return (me_r + shift_r) % n_row, (me_c + shift_c) % n_col
        return (me_r + n_row - shift_r) % n_row, (me_c + n_col - shift_c) % n_col

    barrier = pltpu.get_barrier_semaphore()

    def greet(step, carry):
        pl.semaphore_signal(barrier, inc=1, device_id=peer(step, 1), device_id_type=MESH)
        return carry

    lax.fori_loop(1, devices, greet, 0)

    loads = [
        (slot_h, slot), (offset_h, offset), (forcing_h, forcing), (rate_h, rate), (code_h, code),
        (list_h, listed), (cell_h, cells), (storage_h, storage), (area_h, area),
        (water_h, water), (cap_h, cap), (soil_h, soil), (porosity_h, porosity), (drainage_h, drainage),
    ]
    loads = [pltpu.make_async_copy(a, b, load_sem.at[i]) for i, (a, b) in enumerate(loads)]
    for copy in loads:
        copy.start()
    for copy in loads[:3]:
        copy.wait()
    locate_slots(me_r, me_c, n_row, n_col, slot[...], offset[...], rows, lanes)
    cut_windows(forcing, rows, lanes, weight, windows)

    pl.semaphore_wait(barrier, devices - 1)

    def send_out(step, carry):
        pltpu.make_async_remote_copy(
            src_ref=windows.at[step], dst_ref=arrived.at[me],
            send_sem=out_sem.at[0], recv_sem=out_sem.at[1],
            device_id=peer(step, 1), device_id_type=MESH,
        ).start()
        return carry

    lax.fori_loop(1, devices, send_out, 0)
    arrived[me] = windows[0]

    def neighbour(down, right):
        return (me_r + n_row + down) % n_row, (me_c + n_col + right) % n_col

    routes = [
        (2, (1, 0)), (1, (-1, 0)), (0, (0, 1)), (0, (0, -1)),
        (2, (1, 1)), (2, (1, -1)), (1, (-1, 1)), (1, (-1, -1)),
    ]

    def edge_copies(source, target, sems):
        return [
            pltpu.make_async_remote_copy(
                src_ref=source.at[which], dst_ref=target.at[i],
                send_sem=sems.at[0, i], recv_sem=sems.at[1, i],
                device_id=neighbour(*to), device_id_type=MESH,
            )
            for i, (which, to) in enumerate(routes)
        ]

    loads[3].wait()
    loads[4].wait()
    height = rate.shape[0]
    for first, field in ((0, rate[...]), (8, code[...].astype(f32))):
        at = slice(first, first + 8)
        fixed_edge[0, at, :] = pack_edges(field)
        fixed_edge[1, at, :] = field[:8, :]
        fixed_edge[2, at, :] = field[height - 8 :, :]
    fixed_copies = edge_copies(fixed_edge, fixed_halo, fixed_sem)
    for copy in fixed_copies:
        copy.start()

    loads[5].wait()
    block_pickers(listed[...], pick_rows, pick_slots)
    home_picker(rows, pick_cells)
    loads[6].wait()
    blocks = cells.shape[0]

    def chunk(i):
        return pl.ds(pl.multiple_of(i * CHUNK, CHUNK), CHUNK)

    def tables(i, carry):
        segment_tables(chunk(i), cells, last_of, run)
        return carry

    lax.fori_loop(0, blocks // CHUNK, tables, 0)
    for copy in loads[7:]:
        copy.wait()

    most = pl.ds(0, devices - 1)
    pltpu.make_async_copy(arrived.at[most], arrived.at[most], out_sem.at[1]).wait()
    gather_rows(arrived, pick_rows, parts, found)

    def land(i, carry):
        land_rows(
            chunk(i), found, cells, last_of, run, area, water, cap, canopy, soil, porosity, drainage, sums
        )
        return carry

    lax.fori_loop(0, blocks // CHUNK, land, 0)
    return_rows(pick_slots, sums, leaving)

    def send_back(step, carry):
        to_r, to_c = peer(step, -1)
        pltpu.make_async_remote_copy(
            src_ref=leaving.at[to_r * n_col + to_c], dst_ref=back.at[step],
            send_sem=back_sem.at[0], recv_sem=back_sem.at[1],
            device_id=(to_r, to_c), device_id_type=MESH,
        ).start()
        return carry

    lax.fori_loop(1, devices, send_back, 0)
    back[0] = leaving[me]
    stores = [
        pltpu.make_async_copy(soil, soil_o, store_sem.at[0]),
        pltpu.make_async_copy(canopy, canopy_o, store_sem.at[1]),
    ]
    for copy in stores:
        copy.start()
    for copy in fixed_copies:
        copy.wait()
    pltpu.make_async_copy(windows.at[most], windows.at[most], out_sem.at[0]).wait()

    inside = (me_r > 0, me_r < n_row - 1, me_c > 0, me_c < n_col - 1)
    pltpu.make_async_copy(back.at[most], back.at[most], back_sem.at[1]).wait()
    cell_runoff, cell_evap = place_sums(back, lanes, pick_cells)
    runoff_o[...] = cell_runoff
    evap_o[...] = cell_evap
    river = storage[...] + cell_runoff
    edge[0] = pack_edges(river)
    edge[1] = river[:8, :]
    edge[2] = river[height - 8 :, :]
    edge_sent = edge_copies(edge, halo, edge_sem)
    for copy in edge_sent:
        copy.start()
    whole_rate = extend(rate[...], [fixed_halo[i, 0:8, :] for i in range(8)], inside)
    whole_code = extend(code[...].astype(f32), [fixed_halo[i, 8:16, :] for i in range(8)], inside)
    for copy in edge_sent:
        copy.wait()
    whole = extend(river, [halo[i] for i in range(8)], inside)
    final = route(whole, whole_rate, whole_code)
    river_o[...] = final[8 : 8 + height, :]
    pltpu.make_async_copy(leaving.at[most], leaving.at[most], back_sem.at[0]).wait()
    for copy in stores:
        copy.wait()


def shards(
    forcing, river_storage, river_rate, flow_code, home_slot, home_offset, worker_list,
    patch_cell, patch_area, canopy_water, canopy_cap, soil_water, porosity, drainage,
):
    n_row, n_col = lax.axis_size("region"), lax.axis_size("col")
    devices = n_row * n_col
    grid = river_storage.shape
    slots = home_slot.shape[1]
    blocks = patch_cell.shape[0]
    layers = soil_water.shape[0]
    listed = worker_list.reshape(1, blocks)
    vmem = pltpu.VMEM
    dma = pltpu.SemaphoreType.DMA
    patch = (blocks, LANES)
    scratch = [
        vmem(forcing.shape, f32), vmem(grid, f32), vmem(grid, f32), vmem(grid, i32),
        vmem((1, slots), i32), vmem((1, slots), i32), vmem((1, blocks), i32),
        vmem(patch, i32), vmem(patch, f32), vmem(patch, f32), vmem(patch, f32), vmem(patch, f32),
        vmem((layers,) + patch, f32), vmem((layers,) + patch, f32), vmem((layers,) + patch, f32),
        vmem((slots, LANES), f32), vmem((slots, LANES), i32),
        vmem((2 * LANES, 6 * LANES), bf16),
        vmem((devices, 12, LANES), f32), vmem((devices, 12, LANES), f32),
        vmem((blocks, slots), bf16), vmem((slots, blocks), bf16), vmem((grid[0], slots), bf16),
        vmem(patch, i32), vmem(patch, i32),
        vmem((3, slots, 2 * LANES), bf16), vmem((blocks, 2 * LANES), f32),
        vmem((blocks, 3 * LANES), bf16),
        vmem((devices, 8, LANES), f32), vmem((devices, 8, LANES), f32),
        vmem((3, 16, LANES), f32), vmem((8, 16, LANES), f32),
        vmem((3, 8, LANES), f32), vmem((8, 8, LANES), f32),
        dma((14,)), dma((2,)), dma((2, 8)), dma((2, 8)), dma((2,)), dma((2,)),
    ]
    hbm = pl.BlockSpec(memory_space=pl.ANY)
    near = pl.BlockSpec(memory_space=pltpu.VMEM)
    return pl.pallas_call(
        functools.partial(step_kernel, n_row, n_col),
        out_shape=(
            jax.ShapeDtypeStruct(soil_water.shape, f32),
            jax.ShapeDtypeStruct(patch, f32),
            jax.ShapeDtypeStruct(grid, f32),
            jax.ShapeDtypeStruct(grid, f32),
            jax.ShapeDtypeStruct(grid, f32),
        ),
        in_specs=[hbm] * 14,
        out_specs=(hbm, hbm, near, near, near),
        scratch_shapes=scratch,
        compiler_params=pltpu.CompilerParams(
            collective_id=0, has_side_effects=True, vmem_limit_bytes=56 * 1024 * 1024
        ),
        name="land_step",
    )(
        forcing, river_storage, river_rate, flow_code, home_slot, home_offset, listed,
        patch_cell, patch_area, canopy_water, canopy_cap, soil_water, porosity, drainage,
    )


def solution(mesh):
    both = ("region", "col")
    grid = P("region", "col")
    return jax.shard_map(
        shards,
        mesh=mesh,
        in_specs=(
            P(None, "region", "col"), grid, grid, grid,
            P(both, None), P(both, None), P(both),
            P(both, None), P(both, None), P(both, None), P(both, None),
            P(None, both, None), P(None, both, None), P(None, both, None),
        ),
        out_specs=(P(None, both, None), P(both, None), grid, grid, grid),
        check_vma=False,
    )
```

time: 281 us -> 65.2 us (0.23)
  the two profiles are of different devices: /device:TPU:38 before, /device:TPU:1 now
where the time goes in v1:
time: 65.2 us; the launch traced here: 64.8 us
  Pallas kernels  57.4 us (88%)
  local copies, waits for them, and re-layouts  6.73 us (10%)
  between operations  0.68 us (1%)
    pallas_call x1, Pallas kernels, shards(): pl.pallas_call(functools.partial(step_kernel, n_row, n_col), out_shape=(j...  57.4 us
    unnamed x13, local copies, waits for them, and re-layouts  6.73 us

profile of v1, /device:TPU:1, one launch (start us, length us, event | category | flops | bytes accessed | tf_op | source)
XLA Modules:
  0.0 64.8 jit_solution(12801265232368510949)
XLA Ops:
  0.6 57.4 %land_step.1 = (f32[15,480,128]{2,1,0:T(8,128)}, f32[480,128]{1,0:T(8,128)}, f32[64,128]{1,0:T(8,128)}, f32[64,128]{1,0:T(8,128)}, f32[64,128]{1,0:T(8,128)}) custom-call(f32[3,64,128]{2,1,0:T(8,128)} %forcing_h.1, f32[64,128]{1,0:T(8,128)} %storage_h.1, f32[64,128]{1,0:T(8,128)} %rate_h.1, s32[64,128]{1,0:T(8,128)} %code_h.1, s32[1,1024]{1,0:T(1,128)} %slot_h.1, ...), custom_call_target="tpu_custom_call" | custom-call | tf_op jit(solution)/shard_map/land_step/pallas_call | solution.py:537
  58.0 0.0 copy-start
  58.0 0.0 copy-start.3
  58.0 0.0 copy-start.2
  58.0 0.0 copy-start.1
  58.0 4.2 %copy.24 = f32[15,480,128]{2,1,0:T(8,128)} copy(f32[15,480,128]{2,1,0:T(8,128)} %get-tuple-element.10) | data formatting | bytes 7372800
  62.2 0.0 copy-done
  62.2 0.7 %copy.25 = f32[480,128]{1,0:T(8,128)} copy(f32[480,128]{1,0:T(8,128)S(1)} %copy-done) | data formatting | bytes 491520
  62.9 0.0 copy-done.3
  62.9 0.6 copy.26
  63.5 0.0 copy-done.2
  63.5 0.6 copy.27
  64.2 0.0 copy-done.1
  64.2 0.6 copy.28
Async XLA Ops:
  58.0 4.2 %copy-start = (f32[480,128]{1,0:T(8,128)S(1)}, f32[480,128]{1,0:T(8,128)}, u32[]{:S(2)}) copy-start(f32[480,128]{1,0:T(8,128)} %get-tuple-element.11) | copy-start | bytes 737284
  58.0 4.9 %copy-start.3 = (f32[64,128]{1,0:T(8,128)S(1)}, f32[64,128]{1,0:T(8,128)}, u32[]{:S(2)}) copy-start(f32[64,128]{1,0:T(8,128)} %get-tuple-element.12) | copy-start | bytes 98308
  58.0 5.5 %copy-start.2 = (f32[64,128]{1,0:T(8,128)S(1)}, f32[64,128]{1,0:T(8,128)}, u32[]{:S(2)}) copy-start(f32[64,128]{1,0:T(8,128)} %get-tuple-element.13) | copy-start | bytes 98308
  58.0 6.1 %copy-start.1 = (f32[64,128]{1,0:T(8,128)S(1)}, f32[64,128]{1,0:T(8,128)}, u32[]{:S(2)}) copy-start(f32[64,128]{1,0:T(8,128)} %get-tuple-element.14) | copy-start | bytes 98308

commit v2 on v1

--- a/solution.py
+++ b/solution.py
@@ -344,13 +344,13 @@
     n_col,
     forcing_h, storage_h, rate_h, code_h, slot_h, offset_h, list_h,
     cell_h, area_h, water_h, cap_h, soil_h, porosity_h, drainage_h,
-    soil_o, canopy_o, runoff_o, evap_o, river_o,
+    soil, canopy, runoff_o, evap_o, river_o,
     forcing, storage, rate, code, slot, offset, listed,
-    cells, area, water, cap, canopy, soil, porosity, drainage,
+    cells, area, water, cap, porosity, drainage,
     rows, lanes, weight, windows, arrived, pick_rows, pick_slots, pick_cells,
     last_of, run, parts, found, sums, leaving, back,
     fixed_edge, fixed_halo, edge, halo,
-    load_sem, store_sem, fixed_sem, edge_sem, out_sem, back_sem,
+    load_sem, fixed_sem, edge_sem, out_sem, back_sem,
 ):
     me_r, me_c = lax.axis_index("region"), lax.axis_index("col")
     me = me_r * n_col + me_c
@@ -467,12 +467,6 @@
 
     lax.fori_loop(1, devices, send_back, 0)
     back[0] = leaving[me]
-    stores = [
-        pltpu.make_async_copy(soil, soil_o, store_sem.at[0]),
-        pltpu.make_async_copy(canopy, canopy_o, store_sem.at[1]),
-    ]
-    for copy in stores:
-        copy.start()
     for copy in fixed_copies:
         copy.wait()
     pltpu.make_async_copy(windows.at[most], windows.at[most], out_sem.at[0]).wait()
@@ -497,7 +491,17 @@
     final = route(whole, whole_rate, whole_code)
     river_o[...] = final[8 : 8 + height, :]
     pltpu.make_async_copy(leaving.at[most], leaving.at[most], back_sem.at[0]).wait()
-    for copy in stores:
+
+
+def store_kernel(*refs):
+    count = (len(refs) - 1) // 2
+    sources, targets, sems = refs[:count], refs[count : 2 * count], refs[-1]
+    pairs = [(sources[0].at[l], targets[0].at[l]) for l in range(sources[0].shape[0])]
+    pairs += list(zip(sources[1:], targets[1:]))
+    copies = [pltpu.make_async_copy(a, b, sems.at[i]) for i, (a, b) in enumerate(pairs)]
+    for copy in copies:
+        copy.start()
+    for copy in copies:
         copy.wait()
 
 
@@ -518,8 +522,8 @@
     scratch = [
         vmem(forcing.shape, f32), vmem(grid, f32), vmem(grid, f32), vmem(grid, i32),
         vmem((1, slots), i32), vmem((1, slots), i32), vmem((1, blocks), i32),
-        vmem(patch, i32), vmem(patch, f32), vmem(patch, f32), vmem(patch, f32), vmem(patch, f32),
-        vmem((layers,) + patch, f32), vmem((layers,) + patch, f32), vmem((layers,) + patch, f32),
+        vmem(patch, i32), vmem(patch, f32), vmem(patch, f32), vmem(patch, f32),
+        vmem((layers,) + patch, f32), vmem((layers,) + patch, f32),
         vmem((slots, LANES), f32), vmem((slots, LANES), i32),
         vmem((2 * LANES, 6 * LANES), bf16),
         vmem((devices, 12, LANES), f32), vmem((devices, 12, LANES), f32),
@@ -530,30 +534,35 @@
         vmem((devices, 8, LANES), f32), vmem((devices, 8, LANES), f32),
         vmem((3, 16, LANES), f32), vmem((8, 16, LANES), f32),
         vmem((3, 8, LANES), f32), vmem((8, 8, LANES), f32),
-        dma((14,)), dma((2,)), dma((2, 8)), dma((2, 8)), dma((2,)), dma((2,)),
+        dma((14,)), dma((2, 8)), dma((2, 8)), dma((2,)), dma((2,)),
     ]
-    hbm = pl.BlockSpec(memory_space=pl.ANY)
+    hbm = pl.BlockSpec(memory_space=pltpu.HBM)
     near = pl.BlockSpec(memory_space=pltpu.VMEM)
-    return pl.pallas_call(
+    arguments = (
+        forcing, river_storage, river_rate, flow_code, home_slot, home_offset, listed,
+        patch_cell, patch_area, canopy_water, canopy_cap, soil_water, porosity, drainage,
+    )
+    shapes = (soil_water.shape, patch, grid, grid, grid)
+    results = pl.pallas_call(
         functools.partial(step_kernel, n_row, n_col),
-        out_shape=(
-            jax.ShapeDtypeStruct(soil_water.shape, f32),
-            jax.ShapeDtypeStruct(patch, f32),
-            jax.ShapeDtypeStruct(grid, f32),
-            jax.ShapeDtypeStruct(grid, f32),
-            jax.ShapeDtypeStruct(grid, f32),
-        ),
+        out_shape=tuple(vmem(shape, f32) for shape in shapes),
         in_specs=[hbm] * 14,
-        out_specs=(hbm, hbm, near, near, near),
+        out_specs=(near,) * 5,
         scratch_shapes=scratch,
         compiler_params=pltpu.CompilerParams(
-            collective_id=0, has_side_effects=True, vmem_limit_bytes=56 * 1024 * 1024
+            collective_id=0, has_side_effects=True, vmem_limit_bytes=48 * 1024 * 1024
         ),
         name="land_step",
-    )(
-        forcing, river_storage, river_rate, flow_code, home_slot, home_offset, listed,
-        patch_cell, patch_area, canopy_water, canopy_cap, soil_water, porosity, drainage,
-    )
+    )(*(pltpu.with_memory_space_constraint(value, pltpu.HBM) for value in arguments))
+    return pl.pallas_call(
+        store_kernel,
+        out_shape=tuple(jax.ShapeDtypeStruct(shape, f32) for shape in shapes),
+        in_specs=[near] * 5,
+        out_specs=(hbm,) * 5,
+        scratch_shapes=[dma((layers + 4,))],
+        compiler_params=pltpu.CompilerParams(vmem_limit_bytes=8 * 1024 * 1024),
+        name="store_results",
+    )(*results)
 
 
 def solution(mesh):

time: 65.2 us -> 60.1 us (0.922)
  local copies, waits for them, and re-layouts: 6.73 us -> 0 us
  Pallas kernels: 57.4 us -> 58.9 us
    unnamed x13 -> x0, local copies, waits for them, and re-layouts: 6.73 us -> none
    pallas_call x1 -> x2, Pallas kernels: 57.4 us -> 58.9 us  [the longest x1 56.8 us: shards(): pl.pallas_call(functools.partial(step_kernel, n_row, n_col), out_shape=tu...]
where the time goes in v2:
time: 60.1 us; the launch traced here: 59.6 us
  Pallas kernels  58.9 us (98%)
  between operations  0.65 us (1%)
    pallas_call x1, Pallas kernels, shards(): pl.pallas_call(functools.partial(step_kernel, n_row, n_col), out_shape=tu...  56.8 us
    pallas_call x1, Pallas kernels, shards(): pl.pallas_call(store_kernel, out_shape=tuple((jax.ShapeDtypeStruct(shape,...  2.1 us

profile of v2, /device:TPU:1, one launch (start us, length us, event | category | flops | bytes accessed | tf_op | source)
XLA Modules:
  0.0 59.6 jit_solution(18056444192277561294)
XLA Ops:
  0.6 56.8 %land_step.1 = (f32[15,480,128]{2,1,0:T(8,128)S(1)}, f32[480,128]{1,0:T(8,128)S(1)}, f32[64,128]{1,0:T(8,128)S(1)}, f32[64,128]{1,0:T(8,128)S(1)}, f32[64,128]{1,0:T(8,128)S(1)}) custom-call(f32[3,64,128]{2,1,0:T(8,128)} %forcing_h.1, f32[64,128]{1,0:T(8,128)} %storage_h.1, f32[64,128]{1,0:T(8,128)} %rate_h.1, s32[64,128]{1,0:T(8,128)} %code_h.1, ...), custom_call_target="tpu_custom_call" | custom-call | tf_op jit(solution)/shard_map/land_step/pallas_call | solution.py:546
  57.5 2.1 %store_results.1 = (f32[15,480,128]{2,1,0:T(8,128)}, f32[480,128]{1,0:T(8,128)}, f32[64,128]{1,0:T(8,128)}, f32[64,128]{1,0:T(8,128)}, f32[64,128]{1,0:T(8,128)}) custom-call(f32[15,480,128]{2,1,0:T(8,128)S(1)} %get-tuple-element.10.refs_0_, f32[480,128]{1,0:T(8,128)S(1)} %get-tuple-element.11.refs_1_, f32[64,128]{1,0:T(8,128)S(1)} %get-tuple-element.12.refs_2_, ...), custom_call_target="tpu_custom_call" | custom-call | tf_op jit(solution)/shard_map/store_results/pallas_call | solution.py:557

commit v3 on v2

--- a/solution.py
+++ b/solution.py
@@ -11,7 +11,8 @@
 LANES = 128
 SPAN = 64
 ORDER = 37
-CHUNK = 32
+CHUNK = 96
+QUARTERS = 4
 MESH = pl.DeviceIdType.MESH
 f32, bf16, i32 = jnp.float32, jnp.bfloat16, jnp.int32
 
@@ -66,7 +67,16 @@
     return code // n_col, code % n_col
 
 
-def locate_slots(me_r, me_c, n_row, n_col, slot, offset, rows, lanes):
+def wanted_slots(me_r, me_c, n_row, n_col, sign, index):
+    code = (lax.shift_right_logical(index, 3) * ORDER) & (n_row * n_col - 1)
+    shift_r = lax.shift_right_logical(code, n_col.bit_length() - 1)
+    shift_c = code & (n_col - 1)
+    row = (me_r + n_row + sign * shift_r) & (n_row - 1)
+    column = (me_c + n_col + sign * shift_c) & (n_col - 1)
+    return (row * n_col + column) * 8 + (index & 7)
+
+
+def locate_slots(wanted_at, slot, offset, rows, lanes):
     slots = slot.shape[1]
     part = 2 * LANES
     weight = jnp.where(
@@ -76,13 +86,7 @@
     )
     weight = weight.astype(f32).astype(bf16)
     for first in range(0, slots, part):
-        index = iota((part, LANES), 0) + first
-        step = lax.shift_right_logical(index, 3)
-        code = (step * ORDER) & (n_row * n_col - 1)
-        shift_r = lax.shift_right_logical(code, n_col.bit_length() - 1)
-        shift_c = code & (n_col - 1)
-        worker = ((me_r + shift_r) & (n_row - 1)) * n_col + ((me_c + shift_c) & (n_col - 1))
-        wanted = worker * 8 + (index & 7)
+        wanted = wanted_at(1, iota((part, LANES), 0) + first)
         pick = jnp.concatenate(
             [hot(slot[:, l : l + LANES] == wanted) for l in range(0, slots, LANES)], axis=1
         )
@@ -91,7 +95,7 @@
         lanes[first : first + part, :] = place[:, LANES:].astype(i32)
 
 
-def cut_windows(forcing, rows, lanes, weight, windows):
+def window_weight(forcing, weight):
     grid_rows = forcing.shape[1]
     for v in range(3):
         field = forcing[v]
@@ -101,41 +105,42 @@
             weight[at, v * LANES : (v + 1) * LANES] = a
             weight[at, (3 + v) * LANES : (4 + v) * LANES] = b
     weight[3 * grid_rows :, :] = jnp.zeros((4 * LANES // 2 - 3 * grid_rows, 6 * LANES), bf16)
-    part = 2 * LANES
+
+
+def cut_windows(first, grid_rows, rows, lanes, weight, windows):
+    part = windows.shape[0] * 8 // QUARTERS
     lane = iota((part, LANES), 1)
-    for first in range(0, rows.shape[0], part):
-        at = slice(first, first + part)
-        pick = hot(rows[at, :] == (lane & (grid_rows - 1)).astype(f32))
-        both = dot(jnp.concatenate([pick, pick], axis=1), weight[...])
-        start = lanes[at, :]
-        index = ((lane & (SPAN - 1)) + start) & (LANES - 1)
-        cut = []
-        for v in range(3):
-            near = both[:, v * LANES : (v + 1) * LANES]
-            far = both[:, (3 + v) * LANES : (4 + v) * LANES]
-            cut.append(lane_take(jnp.where(lane >= start, near, far), index))
-        left = lane < SPAN
-        pair = jnp.where(left, cut[0], cut[1])
-        last = jnp.where(left, cut[2], pltpu.roll(cut[2], part - 4, 0))
-        steps = slice(first // 8, (first + part) // 8)
-        windows[steps, 0:8, :] = pair.reshape(part // 8, 8, LANES)
-        windows[steps, 8:12, :] = last.reshape(part // 8, 8, LANES)[:, 0:4, :]
-
-
-def block_pickers(listed, pick_rows, pick_slots):
+    at = slice(first, first + part)
+    pick = hot(rows[at, :] == (lane & (grid_rows - 1)).astype(f32))
+    both = dot(jnp.concatenate([pick, pick], axis=1), weight[...])
+    start = lanes[at, :]
+    index = ((lane & (SPAN - 1)) + start) & (LANES - 1)
+    cut = []
+    for v in range(3):
+        near = both[:, v * LANES : (v + 1) * LANES]
+        far = both[:, (3 + v) * LANES : (4 + v) * LANES]
+        cut.append(lane_take(jnp.where(lane >= start, near, far), index))
+    left = lane < SPAN
+    pair = jnp.where(left, cut[0], cut[1])
+    last = jnp.where(left, cut[2], pltpu.roll(cut[2], part - 4, 0))
+    steps = slice(first // 8, (first + part) // 8)
+    windows[steps, 0:8, :] = pair.reshape(part // 8, 8, LANES)
+    windows[steps, 8:12, :] = last.reshape(part // 8, 8, LANES)[:, 0:4, :]
+
+
+def block_pickers(wanted_at, listed, pick_rows, pick_slots):
     blocks = listed.shape[1]
     slots = pick_slots.shape[0]
     part = 2 * LANES
     for first in range(0, slots, part):
-        row = iota((part, blocks), 0) + first
-        pick_slots[first : first + part, :] = hot(row == listed)
+        wanted = wanted_at(-1, iota((part, 1), 0) + first)
+        pick_slots[first : first + part, :] = hot(wanted == listed)
     for first in range(0, blocks, LANES):
         size = min(LANES, blocks - first)
         column = jnp.broadcast_to(listed[:, first : first + size], (LANES, size)).T
         for l in range(0, slots, LANES):
-            pick_rows[first : first + size, l : l + LANES] = hot(
-                column == iota((size, LANES), 1) + l
-            )
+            wanted = wanted_at(-1, iota((1, LANES), 1) + l)
+            pick_rows[first : first + size, l : l + LANES] = hot(column == wanted)
 
 
 def segment_tables(at, cells, last_of, run):
@@ -154,19 +159,16 @@
     run[at, :] = lane - start
 
 
-def gather_rows(arrived, pick_rows, parts, found):
-    homes = arrived.shape[0]
-    part = 2 * LANES
-    for first in range(0, homes * 8, part):
-        steps = slice(first // 8, (first + part) // 8)
-        pair = arrived[steps, 0:8, :].reshape(part, LANES)
-        half = arrived[steps, 8:12, :]
-        last = jnp.concatenate([half, pltpu.roll(half, SPAN, 2)], axis=1).reshape(part, LANES)
-        for d, (a, b) in enumerate(zip(split3(pair), split3(last))):
-            parts[d, first : first + part, :LANES] = a
-            parts[d, first : first + part, LANES:] = b
-    pick = pick_rows[...]
-    found[...] = dot(pick, parts[0]) + (dot(pick, parts[1]) + dot(pick, parts[2]))
+def gather_rows(first, arrived, pick_rows, found):
+    part = arrived.shape[0] * 8 // QUARTERS
+    steps = slice(first // 8, (first + part) // 8)
+    pair = arrived[steps, 0:8, :].reshape(part, LANES)
+    half = arrived[steps, 8:12, :]
+    last = jnp.concatenate([half, pltpu.roll(half, SPAN, 2)], axis=1).reshape(part, LANES)
+    pick = pick_rows[:, first : first + part]
+    high, middle, low = split3(jnp.concatenate([pair, last], axis=1))
+    rows = dot(pick, high) + (dot(pick, middle) + dot(pick, low))
+    found[...] = rows if first == 0 else found[...] + rows
 
 
 def land_rows(
@@ -189,11 +191,10 @@
     transpired = canopy_loss
     for l in range(layers):
         filled = soil[l, at, :] + flowing
-        excess = jnp.maximum(filled - porosity[l, at, :], 0.0)
-        surface = surface + excess
-        filled = filled - excess
-        flowing = drainage[l, at, :] * filled
-        kept = filled - flowing
+        held = jnp.minimum(filled, porosity[l, at, :])
+        surface = surface + (filled - held)
+        flowing = drainage[l, at, :] * held
+        kept = held - flowing
         if l == 0:
             soil_loss = jnp.minimum(jnp.minimum(soil_demand, demand - canopy_loss), 0.5 * kept)
             kept = kept - soil_loss
@@ -215,12 +216,11 @@
         sums[at, d * LANES : (d + 1) * LANES] = piece
 
 
-def return_rows(pick_slots, sums, leaving):
-    part = 2 * LANES
-    for first in range(0, pick_slots.shape[0], part):
-        three = dot(pick_slots[first : first + part, :], sums[...])
-        total = three[:, :LANES] + (three[:, LANES : 2 * LANES] + three[:, 2 * LANES :])
-        leaving[first // 8 : (first + part) // 8, :, :] = total.reshape(part // 8, 8, LANES)
+def return_rows(first, pick_slots, sums, leaving):
+    part = leaving.shape[0] * 8 // QUARTERS
+    three = dot(pick_slots[first : first + part, :], sums[...])
+    total = three[:, :LANES] + (three[:, LANES : 2 * LANES] + three[:, 2 * LANES :])
+    leaving[first // 8 : (first + part) // 8, :, :] = total.reshape(part // 8, 8, LANES)
 
 
 def home_picker(rows, pick_cells):
@@ -232,34 +232,34 @@
         )
 
 
-def place_sums(back, lanes, pick_cells):
-    part = 2 * LANES
-    grid_rows = pick_cells.shape[0]
+def place_sums(first, back, lanes, pick_cells):
+    part = back.shape[0] * 8 // QUARTERS
     lane = iota((part, LANES), 1)
-    total = jnp.zeros((grid_rows, 4 * LANES), f32)
-    for first in range(0, pick_cells.shape[1], part):
-        at = slice(first, first + part)
-        sent = back[first // 8 : (first + part) // 8, :, :].reshape(part, LANES)
-        start = lanes[at, :]
-        index = (lane - start) & (LANES - 1)
-        inside = index < SPAN
-        near = inside & (lane >= start)
-        far = inside & (lane < start)
-        runoff = lane_take(sent, index)
-        evap = lane_take(sent, (index + SPAN) & (LANES - 1))
-        spread = jnp.concatenate(
-            [
-                jnp.where(near, runoff, 0.0),
-                jnp.where(near, evap, 0.0),
-                jnp.where(far, runoff, 0.0),
-                jnp.where(far, evap, 0.0),
-            ],
-            axis=1,
-        )
-        high, middle, low = split3(spread)
-        pick = pick_cells[:, at]
-        total = total + (dot(pick, high) + (dot(pick, middle) + dot(pick, low)))
-    first_row = iota((grid_rows, 2 * LANES), 0) == 0
+    at = slice(first, first + part)
+    sent = back[first // 8 : (first + part) // 8, :, :].reshape(part, LANES)
+    start = lanes[at, :]
+    index = (lane - start) & (LANES - 1)
+    inside = index < SPAN
+    near = inside & (lane >= start)
+    far = inside & (lane < start)
+    runoff = lane_take(sent, index)
+    evap = lane_take(sent, (index + SPAN) & (LANES - 1))
+    spread = jnp.concatenate(
+        [
+            jnp.where(near, runoff, 0.0),
+            jnp.where(near, evap, 0.0),
+            jnp.where(far, runoff, 0.0),
+            jnp.where(far, evap, 0.0),
+        ],
+        axis=1,
+    )
+    high, middle, low = split3(spread)
+    pick = pick_cells[:, at]
+    return dot(pick, high) + (dot(pick, middle) + dot(pick, low))
+
+
+def cell_sums(total):
+    first_row = iota((total.shape[0], 2 * LANES), 0) == 0
     carried = pltpu.roll(total[:, 2 * LANES :], 1, 0)
     total = total[:, : 2 * LANES] + jnp.where(first_row, 0.0, carried)
     return total[:, :LANES], total[:, LANES:]
@@ -348,13 +348,15 @@
     forcing, storage, rate, code, slot, offset, listed,
     cells, area, water, cap, porosity, drainage,
     rows, lanes, weight, windows, arrived, pick_rows, pick_slots, pick_cells,
-    last_of, run, parts, found, sums, leaving, back,
+    last_of, run, found, sums, leaving, back,
     fixed_edge, fixed_halo, edge, halo,
-    load_sem, fixed_sem, edge_sem, out_sem, back_sem,
+    load_sem, fixed_sem, edge_sem, out_sem, back_sem, arrive_sem, return_sem, ready,
 ):
     me_r, me_c = lax.axis_index("region"), lax.axis_index("col")
-    me = me_r * n_col + me_c
     devices = n_row * n_col
+    steps = devices // QUARTERS
+    quarter = steps * 8
+    wanted_at = functools.partial(wanted_slots, me_r, me_c, n_row, n_col)
 
     def peer(step, sign):
         shift_r, shift_c = step_shift(step, n_row, n_col)
@@ -363,12 +365,10 @@
         return (me_r + n_row - shift_r) % n_row, (me_c + n_col - shift_c) % n_col
 
     barrier = pltpu.get_barrier_semaphore()
-
-    def greet(step, carry):
-        pl.semaphore_signal(barrier, inc=1, device_id=peer(step, 1), device_id_type=MESH)
-        return carry
-
-    lax.fori_loop(1, devices, greet, 0)
+    row_peers = [(me_r, (me_c + i) % n_col) for i in range(1, n_col)]
+    column_peers = [((me_r + i) % n_row, me_c) for i in range(1, n_row)]
+    for to in row_peers + column_peers:
+        pl.semaphore_signal(barrier, inc=1, device_id=to, device_id_type=MESH)
 
     loads = [
         (slot_h, slot), (offset_h, offset), (forcing_h, forcing), (rate_h, rate), (code_h, code),
@@ -380,54 +380,76 @@
         copy.start()
     for copy in loads[:3]:
         copy.wait()
-    locate_slots(me_r, me_c, n_row, n_col, slot[...], offset[...], rows, lanes)
-    cut_windows(forcing, rows, lanes, weight, windows)
-
-    pl.semaphore_wait(barrier, devices - 1)
-
-    def send_out(step, carry):
+    locate_slots(wanted_at, slot[...], offset[...], rows, lanes)
+    pl.semaphore_wait(barrier, n_row + n_col - 2)
+    for to in column_peers:
+        pl.semaphore_signal(ready, inc=1, device_id=to, device_id_type=MESH)
+    height = forcing.shape[1]
+    window_weight(forcing, weight)
+
+    def send_out(part, step, carry):
         pltpu.make_async_remote_copy(
-            src_ref=windows.at[step], dst_ref=arrived.at[me],
-            send_sem=out_sem.at[0], recv_sem=out_sem.at[1],
+            src_ref=windows.at[step], dst_ref=arrived.at[step],
+            send_sem=out_sem.at[0], recv_sem=arrive_sem.at[part],
             device_id=peer(step, 1), device_id_type=MESH,
         ).start()
         return carry
 
-    lax.fori_loop(1, devices, send_out, 0)
-    arrived[me] = windows[0]
-
-    def neighbour(down, right):
-        return (me_r + n_row + down) % n_row, (me_c + n_col + right) % n_col
+    def span(part):
+        first = part * steps if part else 1
+        return first, (part + 1) * steps
+
+    for part in range(QUARTERS):
+        cut_windows(part * quarter, height, rows, lanes, weight, windows)
+        if part == 0:
+            pl.semaphore_wait(ready, n_row - 1)
+        lax.fori_loop(*span(part), functools.partial(send_out, part), 0)
+    arrived[0] = windows[0]
 
     routes = [
         (2, (1, 0)), (1, (-1, 0)), (0, (0, 1)), (0, (0, -1)),
         (2, (1, 1)), (2, (1, -1)), (1, (-1, 1)), (1, (-1, -1)),
     ]
+    row_in = {-1: me_r > 0, 1: me_r < n_row - 1}
+    column_in = {-1: me_c > 0, 1: me_c < n_col - 1}
+
+    def has(down, right):
+        if down and right:
+            return row_in[down] & column_in[right]
+        return row_in[down] if down else column_in[right]
 
     def edge_copies(source, target, sems):
         return [
             pltpu.make_async_remote_copy(
                 src_ref=source.at[which], dst_ref=target.at[i],
                 send_sem=sems.at[0, i], recv_sem=sems.at[1, i],
-                device_id=neighbour(*to), device_id_type=MESH,
+                device_id=((me_r + n_row + down) % n_row, (me_c + n_col + right) % n_col),
+                device_id_type=MESH,
             )
-            for i, (which, to) in enumerate(routes)
+            for i, (which, (down, right)) in enumerate(routes)
         ]
+
+    def start_edges(copies):
+        for copy, (_, (down, right)) in zip(copies, routes):
+            pl.when(has(down, right))(copy.start)
+
+    def wait_edges(copies):
+        for copy, (_, (down, right)) in zip(copies, routes):
+            pl.when(has(down, right))(copy.wait_send)
+            pl.when(has(-down, -right))(copy.wait_recv)
 
     loads[3].wait()
     loads[4].wait()
-    height = rate.shape[0]
     for first, field in ((0, rate[...]), (8, code[...].astype(f32))):
         at = slice(first, first + 8)
         fixed_edge[0, at, :] = pack_edges(field)
         fixed_edge[1, at, :] = field[:8, :]
         fixed_edge[2, at, :] = field[height - 8 :, :]
     fixed_copies = edge_copies(fixed_edge, fixed_halo, fixed_sem)
-    for copy in fixed_copies:
-        copy.start()
+    start_edges(fixed_copies)
 
     loads[5].wait()
-    block_pickers(listed[...], pick_rows, pick_slots)
+    block_pickers(wanted_at, listed[...], pick_rows, pick_slots)
     home_picker(rows, pick_cells)
     loads[6].wait()
     blocks = cells.shape[0]
@@ -443,9 +465,13 @@
     for copy in loads[7:]:
         copy.wait()
 
-    most = pl.ds(0, devices - 1)
-    pltpu.make_async_copy(arrived.at[most], arrived.at[most], out_sem.at[1]).wait()
-    gather_rows(arrived, pick_rows, parts, found)
+    def wait_bytes(buffer, first, last, sem):
+        block = buffer.at[pl.ds(first, last - first)]
+        pltpu.make_async_copy(block, block, sem).wait()
+
+    for part in range(QUARTERS):
+        wait_bytes(arrived, *span(part), arrive_sem.at[part])
+        gather_rows(part * quarter, arrived, pick_rows, found)
 
     def land(i, carry):
         land_rows(
@@ -454,55 +480,60 @@
         return carry
 
     lax.fori_loop(0, blocks // CHUNK, land, 0)
-    return_rows(pick_slots, sums, leaving)
-
-    def send_back(step, carry):
-        to_r, to_c = peer(step, -1)
+
+    def send_back(part, step, carry):
         pltpu.make_async_remote_copy(
-            src_ref=leaving.at[to_r * n_col + to_c], dst_ref=back.at[step],
-            send_sem=back_sem.at[0], recv_sem=back_sem.at[1],
-            device_id=(to_r, to_c), device_id_type=MESH,
+            src_ref=leaving.at[step], dst_ref=back.at[step],
+            send_sem=back_sem.at[0], recv_sem=return_sem.at[part],
+            device_id=peer(step, -1), device_id_type=MESH,
         ).start()
         return carry
 
-    lax.fori_loop(1, devices, send_back, 0)
-    back[0] = leaving[me]
-    for copy in fixed_copies:
-        copy.wait()
-    pltpu.make_async_copy(windows.at[most], windows.at[most], out_sem.at[0]).wait()
-
-    inside = (me_r > 0, me_r < n_row - 1, me_c > 0, me_c < n_col - 1)
-    pltpu.make_async_copy(back.at[most], back.at[most], back_sem.at[1]).wait()
-    cell_runoff, cell_evap = place_sums(back, lanes, pick_cells)
-    runoff_o[...] = cell_runoff
-    evap_o[...] = cell_evap
+    for part in range(QUARTERS):
+        return_rows(part * quarter, pick_slots, sums, leaving)
+        lax.fori_loop(*span(part), functools.partial(send_back, part), 0)
+    back[0] = leaving[0]
+    wait_edges(fixed_copies)
+    inside = (row_in[-1], row_in[1], column_in[-1], column_in[1])
+    for i, field in ((1, rate[...]), (2, code[...].astype(f32))):
+        at = slice(8 * (i - 1), 8 * i)
+        river_o[2 * i], river_o[2 * i + 1] = extend(
+            field, [fixed_halo[j, at, :] for j in range(8)], inside
+        )
+    wait_bytes(windows, 1, devices, out_sem.at[0])
+
+    total = None
+    for part in range(QUARTERS):
+        wait_bytes(back, *span(part), return_sem.at[part])
+        added = place_sums(part * quarter, back, lanes, pick_cells)
+        total = added if total is None else total + added
+    cell_runoff, cell_evap = cell_sums(total)
     river = storage[...] + cell_runoff
     edge[0] = pack_edges(river)
     edge[1] = river[:8, :]
     edge[2] = river[height - 8 :, :]
     edge_sent = edge_copies(edge, halo, edge_sem)
-    for copy in edge_sent:
-        copy.start()
-    whole_rate = extend(rate[...], [fixed_halo[i, 0:8, :] for i in range(8)], inside)
-    whole_code = extend(code[...].astype(f32), [fixed_halo[i, 8:16, :] for i in range(8)], inside)
-    for copy in edge_sent:
-        copy.wait()
-    whole = extend(river, [halo[i] for i in range(8)], inside)
-    final = route(whole, whole_rate, whole_code)
-    river_o[...] = final[8 : 8 + height, :]
-    pltpu.make_async_copy(leaving.at[most], leaving.at[most], back_sem.at[0]).wait()
-
-
-def store_kernel(*refs):
-    count = (len(refs) - 1) // 2
-    sources, targets, sems = refs[:count], refs[count : 2 * count], refs[-1]
-    pairs = [(sources[0].at[l], targets[0].at[l]) for l in range(sources[0].shape[0])]
-    pairs += list(zip(sources[1:], targets[1:]))
+    start_edges(edge_sent)
+    runoff_o[...] = cell_runoff
+    evap_o[...] = cell_evap
+    wait_bytes(leaving, 1, devices, back_sem.at[0])
+    wait_edges(edge_sent)
+    river_o[0], river_o[1] = extend(river, [halo[i] for i in range(8)], inside)
+
+
+def store_kernel(soil, canopy, runoff, evap, tiles, soil_o, canopy_o, runoff_o, evap_o, river_o, river, sems):
+    pairs = [(soil.at[l], soil_o.at[l]) for l in range(soil.shape[0])]
+    pairs += [(canopy, canopy_o), (runoff, runoff_o), (evap, evap_o)]
     copies = [pltpu.make_async_copy(a, b, sems.at[i]) for i, (a, b) in enumerate(pairs)]
     for copy in copies:
         copy.start()
+    final = route((tiles[0], tiles[1]), (tiles[2], tiles[3]), (tiles[4], tiles[5]))
+    river[...] = final[8 : 8 + river.shape[0], :]
+    last = pltpu.make_async_copy(river, river_o, sems.at[len(pairs)])
+    last.start()
     for copy in copies:
         copy.wait()
+    last.wait()
 
 
 def shards(
@@ -529,12 +560,13 @@
         vmem((devices, 12, LANES), f32), vmem((devices, 12, LANES), f32),
         vmem((blocks, slots), bf16), vmem((slots, blocks), bf16), vmem((grid[0], slots), bf16),
         vmem(patch, i32), vmem(patch, i32),
-        vmem((3, slots, 2 * LANES), bf16), vmem((blocks, 2 * LANES), f32),
+        vmem((blocks, 2 * LANES), f32),
         vmem((blocks, 3 * LANES), bf16),
         vmem((devices, 8, LANES), f32), vmem((devices, 8, LANES), f32),
         vmem((3, 16, LANES), f32), vmem((8, 16, LANES), f32),
         vmem((3, 8, LANES), f32), vmem((8, 8, LANES), f32),
-        dma((14,)), dma((2, 8)), dma((2, 8)), dma((2,)), dma((2,)),
+        dma((14,)), dma((2, 8)), dma((2, 8)), dma((1,)), dma((1,)),
+        dma((QUARTERS,)), dma((QUARTERS,)), pltpu.SemaphoreType.REGULAR,
     ]
     hbm = pl.BlockSpec(memory_space=pltpu.HBM)
     near = pl.BlockSpec(memory_space=pltpu.VMEM)
@@ -545,7 +577,7 @@
     shapes = (soil_water.shape, patch, grid, grid, grid)
     results = pl.pallas_call(
         functools.partial(step_kernel, n_row, n_col),
-        out_shape=tuple(vmem(shape, f32) for shape in shapes),
+        out_shape=tuple(vmem(shape, f32) for shape in shapes[:4] + ((6, grid[0] + 16, LANES),)),
         in_specs=[hbm] * 14,
         out_specs=(near,) * 5,
         scratch_shapes=scratch,
@@ -559,7 +591,7 @@
         out_shape=tuple(jax.ShapeDtypeStruct(shape, f32) for shape in shapes),
         in_specs=[near] * 5,
         out_specs=(hbm,) * 5,
-        scratch_shapes=[dma((layers + 4,))],
+        scratch_shapes=[vmem(grid, f32), dma((layers + 4,))],
         compiler_params=pltpu.CompilerParams(vmem_limit_bytes=8 * 1024 * 1024),
         name="store_results",
     )(*results)

time: 60.1 us -> 46.4 us (0.77)
  Pallas kernels: 58.9 us -> 45.7 us
    pallas_call x1, Pallas kernels: 56.8 us -> 43.4 us  [shards(): pl.pallas_call(functools.partial(step_kernel, n_row, n_col), out_shape=tu...]
where the time goes in v3:
time: 46.4 us; the launch traced here: 46.3 us
  Pallas kernels  45.7 us (98%)
  between operations  0.65 us (1%)
    pallas_call x1, Pallas kernels, shards(): pl.pallas_call(functools.partial(step_kernel, n_row, n_col), out_shape=tu...  43.4 us
    pallas_call x1, Pallas kernels, shards(): pl.pallas_call(store_kernel, out_shape=tuple((jax.ShapeDtypeStruct(shape,...  2.27 us

profile of v3, /device:TPU:1, one launch (start us, length us, event | category | flops | bytes accessed | tf_op | source)
XLA Modules:
  0.0 46.3 jit_solution(15145160276967504837)
XLA Ops:
  0.6 43.4 %land_step.1 = (f32[15,480,128]{2,1,0:T(8,128)S(1)}, f32[480,128]{1,0:T(8,128)S(1)}, f32[64,128]{1,0:T(8,128)S(1)}, f32[64,128]{1,0:T(8,128)S(1)}, f32[6,80,128]{2,1,0:T(8,128)S(1)}) custom-call(f32[3,64,128]{2,1,0:T(8,128)} %forcing_h.1, f32[64,128]{1,0:T(8,128)} %storage_h.1, f32[64,128]{1,0:T(8,128)} %rate_h.1, s32[64,128]{1,0:T(8,128)} %code_h.1, ...), custom_call_target="tpu_custom_call" | custom-call | tf_op jit(solution)/shard_map/land_step/pallas_call | solution.py:578
  44.0 2.3 %store_results.1 = (f32[15,480,128]{2,1,0:T(8,128)}, f32[480,128]{1,0:T(8,128)}, f32[64,128]{1,0:T(8,128)}, f32[64,128]{1,0:T(8,128)}, f32[64,128]{1,0:T(8,128)}) custom-call(f32[15,480,128]{2,1,0:T(8,128)S(1)} %get-tuple-element.10.soil, f32[480,128]{1,0:T(8,128)S(1)} %get-tuple-element.11.canopy, f32[64,128]{1,0:T(8,128)S(1)} %get-tuple-element.12.runoff, ...), custom_call_target="tpu_custom_call" | custom-call | tf_op jit(solution)/shard_map/store_results/pallas_call | solution.py:589
